TPU v7x, 768 devices: a whole 4x8x12 slice. The times are simulated.
768 devices in a mesh: shell: 96 (over x, z, core), atom: 8 (over y).
Axes of the slice: x: 4, y: 8, z: 12, core: 2. Of those that a mesh axis runs over, the one named last changes fastest.
Arguments:
- rho: float32 [393216], P('shell'), may hold values from 0.5 to 1.5
- task_point: int32 [96, 768, 256], P('shell', 'atom'), may hold values from 0 to 4095
- task_count: int32 [96, 768], P('shell', 'atom'), may hold values from 1 to 256
- radial_index: int32 [96, 768, 256], P('shell', 'atom'), may hold values from 0 to 126
- fraction: float32 [96, 768, 256], P('shell', 'atom'), may hold values from 0 to 1
- angular: bfloat16 [96, 768, 49, 256], P('shell', 'atom'), may hold values from -6 to 6
- green: float32 [7, 128, 128], replicated, may hold values from -0.0017089844 to 0.0017089844
Outputs:
- potential: float32 [393216], P(('shell', 'atom'))
Inputs may be any that keep to these rules, and one draw needn't show every extreme that they name: Slots j with j >= task_count of their atom and batch are unused.
All inputs are finite; a program needn't handle non-finite values.
Results may differ from a plain program's by a relative error of at most 0.005.
Values may be sent and summed in bfloat16 or wider, within the bound.
No kernel may reach another device: no remote copies, remote signals or barrier semaphores. Data moves between devices by JAX's collectives and lax.ppermute only.
A program may use at most 32 MiB of HBM per device.

v0:
```python
import math

import jax
import jax.numpy as jnp
import numpy as np
from jax import lax
from jax.sharding import PartitionSpec as P

LM = 49
R = 128


green_width_holder = [R]


def split_up(array, dim, peers):
    lengths = array.shape
    blocks = array.reshape(*lengths[:dim], peers, lengths[dim] // peers, *lengths[dim + 1 :])
    return jnp.moveaxis(blocks, dim, 0)


def sent_and_summed(array, axis, dim):
    blocks = split_up(array, dim, lax.axis_size(axis))
    arrived = lax.all_to_all(blocks, axis, split_axis=0, concat_axis=0, tiled=True)
    return arrived.sum(axis=0)


def degree_table():
    return np.array([int(math.isqrt(i)) for i in range(LM)], dtype=np.int32)


def radial_rows(radial_index, fraction):
    width = green_width_holder[0]
    grid = jnp.arange(width, dtype=jnp.int32)
    lower = (grid == radial_index[..., None]).astype(jnp.float32) * (1.0 - fraction)[..., None]
    upper = (grid == radial_index[..., None] + 1).astype(jnp.float32) * fraction[..., None]
    return (lower + upper).astype(jnp.bfloat16)


def radial_solve(moments, green):
    kernels = green[degree_table()]
    return jnp.einsum("alq,lqr->alr", moments, kernels, precision=lax.Precision.HIGHEST).astype(
        jnp.bfloat16
    )


def per_device(rho, task_point, task_count, radial_index, fraction, angular, green):
    points = task_point[0]
    counts = task_count[0]
    angles = angular[0]
    slot_ids = jnp.arange(points.shape[1], dtype=jnp.int32)
    live = (slot_ids[None, :] < counts[:, None]).astype(jnp.float32)
    picked = rho[points] * live
    weighted = (angles.astype(jnp.float32) * picked[:, None, :]).astype(jnp.bfloat16)
    rows = radial_rows(radial_index[0], fraction[0])
    partial_value = jnp.einsum("als,asr->alr", weighted, rows, preferred_element_type=jnp.float32)
    moments = lax.psum(partial_value, "shell")
    table = radial_solve(moments, green)
    radial = jnp.einsum("alr,asr->als", table, rows, preferred_element_type=jnp.float32)
    values = jnp.sum(angles.astype(jnp.float32) * radial, axis=1) * live
    terms = jnp.zeros((rho.shape[0],), jnp.float32).at[points.reshape(-1)].add(values.reshape(-1))
    return sent_and_summed(terms, "atom", 0)


def solution(mesh):
    in_specs = (
        P("shell"),
        P("shell", "atom", None),
        P("shell", "atom"),
        P("shell", "atom", None),
        P("shell", "atom", None),
        P("shell", "atom", None, None),
        P(),
    )
    out_specs = P(("shell", "atom"))
    return jax.shard_map(
        per_device, mesh=mesh, in_specs=in_specs, out_specs=out_specs, check_vma=False
    )
```

profile of v0, /device:TPU:1, one launch (start us, length us, event | category | flops | bytes accessed | tf_op | source)
XLA Modules:
  0.0 635.8 jit_solution(9627822949245316365)
XLA Ops:
  6.5 0.0 copy-start
  6.5 0.0 all-reduce.2.cloned.1.call-start
  6.5 1.0 fusion.17
  7.5 0.1 copy.21
  7.6 0.0 copy-done.1
  7.6 0.0 copy-start.3
  7.6 0.0 copy-start.4
  7.6 0.0 copy-start.5
  7.6 0.0 copy-start.7
  7.7 135.5 %gather_fusion.1 = f32[24576]{0:T(1024)S(1)} fusion(f32[4096]{0:T(1024)S(1)} %copy-done.1, s32[24576]{0:T(1024)S(1)} %broadcast_clamp_fusion), kind=kCustom, calls=%fused_computation.1 | custom fusion | bytes 294912 | tf_op jit(solution)/shard_map/gather | solution.py:53
  143.2 0.0 copy-done.3
  143.3 0.0 copy-done.4
  143.3 0.0 copy-done.5
  143.3 0.1 fusion.18
  143.4 0.0 copy-done.7
  143.4 0.0 copy-start.2
  143.4 0.0 copy-start.6
  143.4 20.8 %fusion.1 = f32[96,49,128]{2,1,0:T(8,128)} fusion(f32[96,256]{1,0:T(8,128)S(1)} %bitcast.40, s32[96,256]{1,0:T(8,128)S(1)} %broadcast_add_fusion, f32[96,256]{1,0:T(8,128)S(1)} %get-tuple-element.6, s32[96,256]{1,0:T(8,128)S(1)} %bitcast.36, f32[96,256]{1,0:T(8,128)S(1)} %get-tuple-element.5, bf16[1,96,49,256]{3,1,2,0:T(8,128)(2,1)S(1)} %copy-done.7), kind=kOutput, calls=%fused_computation.9 | convolution fusion | flops 330768384 | bytes 5308416 | tf_op jit(solution)/shard_map/als,asr->alr/dot_general | solution.py:56
  164.2 0.0 all-reduce.2.cloned.1.call-update
  164.2 0.0 copy-done.2
  164.2 0.1 copy.20
  164.4 0.1 compare_select_fusion
  164.5 0.0 copy-done
  164.5 2.4 gather_fusion
  166.9 293.9 %all-reduce.2.cloned.1.call-done = f32[96,49,128]{2,1,0:T(8,128)} async-done(((f32[96,49,128]{2,1,0:T(8,128)}), f32[96,49,128]{2,1,0:T(8,128)}) %all-reduce.2.cloned.1.call-update) | async-done | bytes 2408464 | tf_op jit(solution)/shard_map/psum | solution.py:57
  460.8 5.9 fusion.13
  466.7 20.2 %fusion.3 = f32[96,256]{1,0:T(8,128)S(1)} fusion(bf16[1,96,49,256]{3,1,2,0:T(8,128)(2,1)S(1)} %copy-done.7, f32[96,256]{1,0:T(8,128)S(1)} %bitcast.41, s32[96,256]{1,0:T(8,128)S(1)} %broadcast_add_fusion, f32[96,256]{1,0:T(8,128)S(1)} %get-tuple-element.6, s32[96,256]{1,0:T(8,128)S(1)} %bitcast.37, bf16[96,49,128]{2,0,1:T(8,128)(2,1)S(1)} %fusion.13), kind=kOutput, calls=%fused_computation.11 | convolution fusion | flops 330743808 | bytes 4104192 | tf_op jit(solution)/shard_map/alr,asr->als/dot_general | solution.py:59
  486.9 0.1 select_bitcast_fusion
  487.0 0.1 copy.22
  487.0 128.4 %scatter_custom_fusion = f32[4096]{0:T(1024)S(1)} fusion(s32[24576]{0:T(1024)S(1)} %bitcast.38, f32[24576]{0:T(1024)S(1)} %bitcast.39, f32[]{:T(128)} %constant.8.clone.1), kind=kCustom, calls=%fused_computation.29 | custom fusion | flops 24576 | bytes 16388 | tf_op jit(solution)/shard_map/scatter-add | solution.py:61
  615.5 12.9 %all_to_all.9 = f32[8,1,512]{2,1,0:T(1,128)S(1)} all-to-all(f32[8,1,512]{2,1,0:T(1,128)S(1)} %bitcast.42), channel_id=1, replica_groups=mesh['shell'=96,'atom'=8] {'atom'}, dimensions={0} | all-to-all | bytes 32768 | tf_op jit(solution)/shard_map/all_to_all | solution.py:24
  628.4 0.6 reduce_sum.19
  (6 shorter events, 0.1 us)
Async XLA Ops:
  6.5 158.0 %copy-start = (f32[7,128,128]{2,1,0:T(8,128)S(1)}, f32[7,128,128]{2,1,0:T(8,128)}, u32[]{:S(2)}) copy-start(f32[7,128,128]{2,1,0:T(8,128)} %param.15) | copy-start | bytes 1376260
  6.5 1.1 copy-start.1
  6.5 454.3 %all-reduce.2.cloned.1.call-start = ((), (), s32[]{:S(2)}) async-start(), calls=%async_computation.1 | async-start | bytes 5505024 | tf_op jit(solution)/shard_map/psum | solution.py:57
  7.6 135.6 %copy-start.3 = (s32[1,96,256]{2,1,0:T(8,128)S(1)}, s32[1,96,256]{2,1,0:T(8,128)}, u32[]{:S(2)}) copy-start(s32[1,96,256]{2,1,0:T(8,128)} %param.12) | copy-start | bytes 294916
  7.6 135.6 %copy-start.4 = (f32[1,96,256]{2,1,0:T(8,128)S(1)}, f32[1,96,256]{2,1,0:T(8,128)}, u32[]{:S(2)}) copy-start(f32[1,96,256]{2,1,0:T(8,128)} %param.13) | copy-start | bytes 294916
  7.6 135.6 %copy-start.5 = (s32[1,96]{1,0:T(1,128)S(1)}, s32[1,96]{1,0:T(1,128)}, u32[]{:S(2)}) copy-start(s32[1,96]{1,0:T(1,128)} %param.11) | copy-start | bytes 1156
  7.6 135.7 %copy-start.7 = (bf16[1,96,49,256]{3,1,2,0:T(8,128)(2,1)S(1)}, bf16[1,96,49,256]{3,1,2,0:T(8,128)(2,1)}, u32[]{:S(2)}) copy-start(bf16[1,96,49,256]{3,1,2,0:T(8,128)(2,1)} %param.14) | copy-start | bytes 7225348
  143.4 20.9 %copy-start.2 = (s32[1,96,256]{2,1,0:T(8,128)S(1)}, s32[1,96,256]{2,1,0:T(8,128)}, u32[]{:S(2)}) copy-start(s32[1,96,256]{2,1,0:T(8,128)} %param.10) | copy-start | bytes 294916
  143.4 21.1 %copy-start.6 = (s32[49]{0:T(128)S(1)}, s32[49]{0:T(128)}, u32[]{:S(2)}) copy-start(s32[49]{0:T(128)} %constant.32) | copy-start | bytes 592
Sparse Core Ops, SparseCore 0:
  164.4 296.4 all-reduce.1
where the time goes:
time: 636 us
  waiting for transfers between devices  294 us (46%)
  local copies, waits for them, and re-layouts  138 us (22%)
  other arithmetic  130 us (20%)
  matrix products  46.8 us (7%)
  between operations  13.6 us (2%)
  blocking collectives  12.9 us (2%)
    psum x1, waiting for transfers between devices, per_device(): moments = lax.psum(partial_value, 'shell')  294 us
    gather x2, local copies, waits for them, and re-layouts, per_device(): picked = rho[points] * live  136 us
    scatter-add x1, other arithmetic, per_device(): jnp.zeros((rho.shape[0],), jnp.float32).at[points.reshape(-1)]  128 us
    dot_general x1, matrix products, per_device(): jnp.einsum('als,asr->alr', weighted, rows, preferred_element_type=jnp.flo...  20.8 us
    dot_general x1, matrix products, per_device(): jnp.einsum('alr,asr->als', table, rows, preferred_element_type=jnp.float32)  20.2 us
    all_to_all x1, blocking collectives, sent_and_summed(): lax.all_to_all(blocks, axis, split_axis=0, concat_axis=0, tiled=True)  12.9 us
  transfers between devices with their start and end apart: 1, of which 1 were waited for; matrix products, arithmetic and copies ran while one was open for 0% of the time, Pallas kernels for 0%

commit v1 on v0

v1 whole, which is shorter than its diff:
```python
import jax
import jax.numpy as jnp
from jax import lax
from jax.experimental import pallas as pl
from jax.experimental.pallas import tpu as pltpu
from jax.sharding import Mesh, PartitionSpec as P

X, Z, CORES = 4, 12, 2
LMAX = 6
LM = 49
ROWS = 56
R = 128
SLOTS = 256
PTS = 4096
HALF = 48
BLOCK = 8
STEPS = HALF // BLOCK
HIGH, LOW = 32, 128

f32 = jnp.float32
bf16 = jnp.bfloat16


def hat_rows(index, fraction):
    grid = lax.broadcasted_iota(jnp.int32, (R, SLOTS), 0)
    upper = jnp.where(grid == index + 1, fraction, 0.0)
    return jnp.where(grid == index, 1.0 - fraction, upper).astype(bf16)


def one_hot_low(points):
    grid = lax.broadcasted_iota(jnp.int32, (LOW, SLOTS), 0)
    return jnp.where(grid == (points & (LOW - 1)), 1.0, 0.0).astype(bf16)


def is_high(points):
    return lax.broadcasted_iota(jnp.int32, (HIGH, SLOTS), 0) == lax.shift_right_logical(points, 7)


def moments_kernel(half_ref, count_ref, rho_ref, point_ref, index_ref, fraction_ref, angular_ref, out_ref, weighted_ref):
    first = (half_ref[0] * STEPS + pl.program_id(0)) * BLOCK
    rho = rho_ref[...]
    big = rho.astype(bf16)
    small = (rho - big.astype(f32)).astype(bf16)
    rho_parts = jnp.concatenate([big, small], axis=1)
    slot = lax.broadcasted_iota(jnp.int32, (1, SLOTS), 1)
    densities = []
    for i in range(BLOCK):
        points = point_ref[i : i + 1, :]
        low = one_hot_low(points)
        columns = jnp.dot(rho_parts, jnp.concatenate([low, low], axis=0), preferred_element_type=f32)
        picked = jnp.sum(jnp.where(is_high(points), columns, 0.0), axis=0, keepdims=True)
        densities.append(jnp.where(slot < count_ref[first + i], picked, 0.0))
    densities = jnp.concatenate(densities, axis=0)
    for m in range(LM):
        weighted_ref[m] = angular_ref[m].astype(f32) * densities
    weighted_ref[LM:] = jnp.zeros((ROWS - LM, BLOCK, SLOTS), f32)
    for i in range(BLOCK):
        rows = hat_rows(index_ref[i : i + 1, :], fraction_ref[i : i + 1, :])
        out_ref[i] = lax.dot_general(
            weighted_ref[:, i, :].astype(bf16), rows, (((1,), (1,)), ((), ())), preferred_element_type=f32
        ).astype(bf16)


def evaluate_kernel(half_ref, count_ref, table_ref, point_ref, index_ref, fraction_ref, angular_ref, out_ref, sum_ref, radial_ref):
    first = (half_ref[0] * STEPS + pl.program_id(0)) * BLOCK
    slot = lax.broadcasted_iota(jnp.int32, (1, SLOTS), 1)

    @pl.when(pl.program_id(0) == 0)
    def _():
        sum_ref[...] = jnp.zeros_like(sum_ref)

    for i in range(BLOCK):
        rows = hat_rows(index_ref[i : i + 1, :], fraction_ref[i : i + 1, :])
        radial_ref[:, i, :] = jnp.dot(table_ref[i], rows, preferred_element_type=f32)
    values = angular_ref[0].astype(f32) * radial_ref[0]
    for m in range(1, LM):
        values = values + angular_ref[m].astype(f32) * radial_ref[m]
    total = sum_ref[...]
    for i in range(BLOCK):
        points = point_ref[i : i + 1, :]
        value = jnp.where(slot < count_ref[first + i], values[i : i + 1, :], 0.0)
        big = value.astype(bf16).astype(f32)
        small = value - big
        high = is_high(points)
        spread = jnp.concatenate([jnp.where(high, big, 0.0), jnp.where(high, small, 0.0)], axis=0)
        total = total + lax.dot_general(
            spread.astype(bf16), one_hot_low(points), (((1,), (1,)), ((), ())), preferred_element_type=f32
        )
    sum_ref[...] = total

    @pl.when(pl.program_id(0) == STEPS - 1)
    def _():
        out_ref[...] = total[:HIGH] + total[HIGH:]


def solve_kernel(parts_ref, green_ref, table_ref):
    moments = jnp.sum(parts_ref[...].astype(f32), axis=0)
    row = lax.broadcasted_iota(jnp.int32, (ROWS, R), 0)
    table = jnp.zeros((ROWS, R), f32)
    for degree in range(LMAX + 1):
        of_degree = (row >= degree * degree) & (row < (degree + 1) * (degree + 1))
        table = table + jnp.dot(
            jnp.where(of_degree, moments, 0.0), green_ref[degree], precision=lax.Precision.HIGHEST, preferred_element_type=f32
        )
    table_ref[...] = table.astype(bf16)


def task_block(half_of):
    return pl.BlockSpec((BLOCK, SLOTS), lambda step, half, count: (half[0] * STEPS + step, 0))


def angular_block():
    return pl.BlockSpec((LM, BLOCK, SLOTS), lambda step, half, count: (0, half[0] * STEPS + step, 0))


def moments_of(half, count, rho, points, index, fraction, angular):
    return pl.pallas_call(
        moments_kernel,
        out_shape=jax.ShapeDtypeStruct((HALF, ROWS, R), bf16),
        grid_spec=pltpu.PrefetchScalarGridSpec(
            num_scalar_prefetch=2,
            grid=(STEPS,),
            in_specs=[pl.BlockSpec((HIGH, LOW), lambda step, half, count: (0, 0))]
            + [task_block(half)] * 3
            + [angular_block()],
            out_specs=pl.BlockSpec((BLOCK, ROWS, R), lambda step, half, count: (step, 0, 0)),
            scratch_shapes=[pltpu.VMEM((ROWS, BLOCK, SLOTS), f32)],
        ),
        name="moments",
    )(half, count, rho, points, index, fraction, angular)


def evaluated(half, count, table, points, index, fraction, angular):
    return pl.pallas_call(
        evaluate_kernel,
        out_shape=jax.ShapeDtypeStruct((HIGH, LOW), f32),
        grid_spec=pltpu.PrefetchScalarGridSpec(
            num_scalar_prefetch=2,
            grid=(STEPS,),
            in_specs=[pl.BlockSpec((BLOCK, ROWS, R), lambda step, half, count: (step, 0, 0))]
            + [task_block(half)] * 3
            + [angular_block()],
            out_specs=pl.BlockSpec((HIGH, LOW), lambda step, half, count: (0, 0)),
            scratch_shapes=[pltpu.VMEM((2 * HIGH, LOW), f32), pltpu.VMEM((ROWS, BLOCK, SLOTS), f32)],
        ),
        name="evaluate",
    )(half, count, table, points, index, fraction, angular)


def solved(parts, green):
    return pl.pallas_call(
        solve_kernel,
        out_shape=jax.ShapeDtypeStruct((ROWS, R), bf16),
        name="solve",
    )(parts, green)


def exchanged(array, axis):
    return lax.all_to_all(array, axis, split_axis=0, concat_axis=0, tiled=True)


def to_other_core(array):
    return lax.ppermute(array, "core", [(0, 1), (1, 0)])


def per_device(rho, task_point, task_count, radial_index, fraction, angular, green):
    core = lax.axis_index("core")
    own = core.astype(jnp.int32).reshape(1)
    other = 1 - own
    tasks = (task_point[0], radial_index[0], fraction[0], angular[0].transpose(1, 0, 2))
    count = task_count[0]
    rho = rho.reshape(HIGH, LOW)

    sent = moments_of(other, count, rho, *tasks)
    arrived = to_other_core(sent)
    kept = moments_of(own, count, rho, *tasks)
    chip = (kept.astype(f32) + arrived.astype(f32)).astype(bf16)
    along_x = exchanged(chip.reshape(X, Z, ROWS, R), "x")
    plane = along_x.astype(f32).sum(axis=0).astype(bf16)
    parts = exchanged(plane, "z")
    table = solved(parts, green)

    column = exchanged(jnp.broadcast_to(table, (Z, ROWS, R)), "z")
    half = exchanged(jnp.broadcast_to(column, (X, Z, ROWS, R)), "x").reshape(HALF, ROWS, R)
    other_half = to_other_core(half)
    terms = evaluated(own, count, half, *tasks)
    terms = terms + evaluated(other, count, other_half, *tasks)
    return exchanged(terms.reshape(8, PTS // 8), "atom").sum(axis=0)


def solution(mesh):
    mesh = Mesh(mesh.devices.reshape(X, Z, CORES, 8), ("x", "z", "core", "atom"))
    shell = ("x", "z", "core")
    in_specs = (
        P(shell),
        P(shell, "atom", None),
        P(shell, "atom"),
        P(shell, "atom", None),
        P(shell, "atom", None),
        P(shell, "atom", None, None),
        P(),
    )
    return jax.shard_map(
        per_device, mesh=mesh, in_specs=in_specs, out_specs=P((*shell, "atom")), check_vma=False
    )
```

time: 636 us -> 129 us (0.20)
  waiting for transfers between devices: 294 us -> 0.01 us
  local copies, waits for them, and re-layouts: 138 us -> 1.68 us
  other arithmetic: 130 us -> 2.71 us
  blocking collectives: 12.9 us -> 69.2 us
  matrix products: 46.8 us -> 0 us
  Pallas kernels: 0 us -> 34.9 us
  starting transfers between devices: 0.01 us -> 19.6 us
  between operations: 13.6 us -> 0.06 us
    psum x1 -> x0, waiting for transfers between devices: 294 us -> none  [per_device(): moments = lax.psum(partial_value, 'shell')]
    gather x3 -> x0, local copies, waits for them, and re-layouts: 138 us -> none  [the longest x2 136 us: per_device(): picked = rho[points] * live]
    scatter-add x1 -> x0, other arithmetic: 128 us -> none  [per_device(): jnp.zeros((rho.shape[0],), jnp.float32).at[points.reshape(-1)]]
    all_to_all x1 -> x5, blocking collectives: 12.9 us -> 69.2 us  [exchanged(): return lax.all_to_all(array, axis, split_axis=0, concat_axis=0, tiled=True)]
    dot_general x3 -> x0, matrix products: 46.8 us -> none  [the longest x1 20.8 us: per_device(): jnp.einsum('als,asr->alr', weighted, rows, preferred_element_type=jnp.flo...]
    pallas_call x0 -> x5, Pallas kernels: none -> 34.9 us  [the longest x2 18.1 us: moments_of(): pl.pallas_call(moments_kernel, out_shape=jax.ShapeDtypeStruct((HALF, ROWS...]
    ppermute x0 -> x2, starting transfers between devices: none -> 19.6 us  [to_other_core(): return lax.ppermute(array, 'core', [(0, 1), (1, 0)])]
  transfers between devices with their start and end apart: 1 -> 2, of which waited for: 1 -> 0; matrix products, arithmetic and copies ran while one was open for 0% -> 0% of each run, Pallas kernels for 0% -> 13%
where the time goes in v1:
time: 129 us; the launch traced here: 128 us
  blocking collectives  69.2 us (54%)
  Pallas kernels  34.9 us (27%)
  starting transfers between devices  19.6 us (15%)
  other arithmetic  2.71 us (2%)
  local copies, waits for them, and re-layouts  1.68 us (1%)
    all_to_all x5, blocking collectives, exchanged(): return lax.all_to_all(array, axis, split_axis=0, concat_axis=0, tiled=True)  69.2 us
    ppermute x2, starting transfers between devices, to_other_core(): return lax.ppermute(array, 'core', [(0, 1), (1, 0)])  19.6 us
    pallas_call x2, Pallas kernels, moments_of(): pl.pallas_call(moments_kernel, out_shape=jax.ShapeDtypeStruct((HALF, ROWS...  18.1 us
    pallas_call x2, Pallas kernels, evaluated(): pl.pallas_call(evaluate_kernel, out_shape=jax.ShapeDtypeStruct((HIGH, LOW...  14.6 us
  transfers between devices with their start and end apart: 2, of which 0 were waited for; matrix products, arithmetic and copies ran while one was open for 0% of the time, Pallas kernels for 13%

profile of v1, /device:TPU:1, one launch (start us, length us, event | category | flops | bytes accessed | tf_op | source)
XLA Modules:
  0.0 128.2 jit_solution(15308445224406071079)
XLA Ops:
  0.0 9.0 %moments.3 = bf16[48,56,128]{2,1,0:T(8,128)(2,1)} custom-call(s32[1]{0:T(128)S(6)} %sub.3.half_ref, s32[96]{0:T(128)} %bitcast.34, f32[32,128]{1,0:T(8,128)} %bitcast.31, s32[96,256]{1,0:T(8,128)} %bitcast.19, s32[96,256]{1,0:T(8,128)} %bitcast.23, f32[96,256]{1,0:T(8,128)} %bitcast.27, bf16[49,96,256]{2,1,0:T(8,128)(2,1)} %bitcast.12), custom_call_target="tpu_custom_call" | custom-call | tf_op jit(solution)/shard_map/moments/pallas_call | solution.py:117
  9.0 12.4 %collective-permute-start = (bf16[48,56,128]{2,1,0:T(8,128)(2,1)}, bf16[48,56,128]{2,1,0:T(8,128)(2,1)S(1)}, u32[]{:S(2)}, u32[]{:S(2)}) collective-permute-start(bf16[48,56,128]{2,1,0:T(8,128)(2,1)} %moments.3), channel_id=1, source_target_pairs={{0,8},{8,0},{1,9},{9,1},{2,10},{10,2},{3,11},{11,3},{4,12},{12,4},... | collective-permute-start | bytes 2064392 | tf_op jit(solution)/shard_map/ppermute | solution.py:163
  21.4 9.0 %moments.2 = bf16[48,56,128]{2,1,0:T(8,128)(2,1)} custom-call(s32[1]{0:T(128)} %bitcast.half_ref, s32[96]{0:T(128)} %bitcast.35, f32[32,128]{1,0:T(8,128)} %bitcast.32, s32[96,256]{1,0:T(8,128)} %bitcast.20, s32[96,256]{1,0:T(8,128)} %bitcast.24, f32[96,256]{1,0:T(8,128)} %bitcast.28, bf16[49,96,256]{2,1,0:T(8,128)(2,1)} %bitcast.13), custom_call_target="tpu_custom_call" | custom-call | tf_op jit(solution)/shard_map/moments/pallas_call | solution.py:117
  30.5 0.0 collective-permute-done
  30.5 1.3 add_convert_fusion
  31.7 13.7 %all_to_all.29 = bf16[4,12,56,128]{3,2,1,0:T(8,128)(2,1)S(1)} all-to-all(bf16[4,12,56,128]{3,2,1,0:T(8,128)(2,1)S(1)} %bitcast.18), channel_id=1, replica_groups=mesh['x'=4,'z'=12,'core'=2,'atom'=8] {'x'}, dimensions={0} | all-to-all | bytes 1376256 | tf_op jit(solution)/shard_map/all_to_all | solution.py:159
  45.4 0.1 reduce_sum.21
  45.6 17.5 %all_to_all.30.parts_ref = bf16[12,56,128]{2,1,0:T(8,128)(2,1)} all-to-all(bf16[12,56,128]{2,1,0:T(8,128)(2,1)S(1)} %reduce_sum.21), channel_id=1, replica_groups=mesh['x'=4,'z'=12,'core'=2,'atom'=8] {'z'}, dimensions={0} | all-to-all | bytes 344064 | tf_op jit(solution)/shard_map/all_to_all | solution.py:159
  63.0 2.2 %solve.1 = bf16[56,128]{1,0:T(8,128)(2,1)} custom-call(bf16[12,56,128]{2,1,0:T(8,128)(2,1)} %all_to_all.30.parts_ref, f32[7,128,128]{2,1,0:T(8,128)} %green_ref.1), custom_call_target="tpu_custom_call" | custom-call | tf_op jit(solution)/shard_map/solve/pallas_call | solution.py:151
  65.3 0.7 broadcast_in_dim.6
  66.0 14.6 %all_to_all.31 = bf16[12,56,128]{2,1,0:T(8,128)(2,1)S(1)} all-to-all(bf16[12,56,128]{2,1,0:T(8,128)(2,1)S(1)} %broadcast_in_dim.6), channel_id=1, replica_groups=mesh['x'=4,'z'=12,'core'=2,'atom'=8] {'z'}, dimensions={0} | all-to-all | bytes 344064 | tf_op jit(solution)/shard_map/all_to_all | solution.py:159
  80.6 0.1 broadcast_in_dim.7
  80.7 10.2 %all_to_all.32 = bf16[4,12,56,128]{3,2,1,0:T(8,128)(2,1)S(1)} all-to-all(bf16[4,12,56,128]{3,2,1,0:T(8,128)(2,1)S(1)} %broadcast_in_dim.7), channel_id=1, replica_groups=mesh['x'=4,'z'=12,'core'=2,'atom'=8] {'x'}, dimensions={0} | all-to-all | bytes 1376256 | tf_op jit(solution)/shard_map/all_to_all | solution.py:159
  90.9 0.0 copy-start
  90.9 7.2 %collective-permute-start.1 = (bf16[48,56,128]{2,1,0:T(8,128)(2,1)S(1)}, bf16[48,56,128]{2,1,0:T(8,128)(2,1)S(1)}, u32[]{:S(2)}, u32[]{:S(2)}) collective-permute-start(bf16[48,56,128]{2,1,0:T(8,128)(2,1)S(1)} %bitcast.16), channel_id=1, source_target_pairs={{0,8},{8,0},{1,9},{9,1},{2,10},{10,2},{3,11},{11,3},{4,12},{12,4},... | collective-permute-start | bytes 2064392 | tf_op jit(solution)/shard_map/ppermute | solution.py:163
  98.1 0.0 copy-done
  98.1 7.3 %evaluate.2 = f32[32,128]{1,0:T(8,128)} custom-call(s32[1]{0:T(128)} %bitcast.half_ref, s32[96]{0:T(128)} %bitcast.36, bf16[48,56,128]{2,1,0:T(8,128)(2,1)} %bitcast.17, s32[96,256]{1,0:T(8,128)} %bitcast.21, s32[96,256]{1,0:T(8,128)} %bitcast.25, f32[96,256]{1,0:T(8,128)} %bitcast.29, bf16[49,96,256]{2,1,0:T(8,128)(2,1)} %bitcast.14), custom_call_target="tpu_custom_call" | custom-call | tf_op jit(solution)/shard_map/evaluate/pallas_call | solution.py:134
  105.5 0.0 copy-start.2
  105.5 0.0 collective-permute-done.1.table_ref
  105.5 0.0 copy-start.1
  105.5 0.8 copy-done.1
  106.3 7.3 %evaluate.3 = f32[32,128]{1,0:T(8,128)} custom-call(s32[1]{0:T(128)S(6)} %sub.3.half_ref, s32[96]{0:T(128)} %bitcast.37, bf16[48,56,128]{2,1,0:T(8,128)(2,1)} %copy-done.1, s32[96,256]{1,0:T(8,128)} %bitcast.22, s32[96,256]{1,0:T(8,128)} %bitcast.26, f32[96,256]{1,0:T(8,128)} %bitcast.30, bf16[49,96,256]{2,1,0:T(8,128)(2,1)} %bitcast.15), custom_call_target="tpu_custom_call" | custom-call | tf_op jit(solution)/shard_map/evaluate/pallas_call | solution.py:134
  113.6 0.0 copy-done.2
  113.6 0.7 add.7
  114.4 13.2 %all_to_all.33 = f32[8,1,512]{2,1,0:T(1,128)S(1)} all-to-all(f32[8,1,512]{2,1,0:T(1,128)S(1)} %bitcast.33), channel_id=1, replica_groups=mesh['x'=4,'z'=12,'core'=2,'atom'=8] {'atom'}, dimensions={0} | all-to-all | bytes 32768 | tf_op jit(solution)/shard_map/all_to_all | solution.py:159
  127.6 0.6 reduce_sum.22
Async XLA Ops:
  9.0 21.4 %collective-permute-start = (bf16[48,56,128]{2,1,0:T(8,128)(2,1)}, bf16[48,56,128]{2,1,0:T(8,128)(2,1)S(1)}, u32[]{:S(2)}, u32[]{:S(2)}) collective-permute-start(bf16[48,56,128]{2,1,0:T(8,128)(2,1)} %moments.3), channel_id=1, source_target_pairs={{0,8},{8,0},{1,9},{9,1},{2,10},{10,2},{3,11},{11,3},{4,12},{12,4},... | collective-permute-start | bytes 2064392 | tf_op jit(solution)/shard_map/ppermute | solution.py:163
  90.9 7.3 %copy-start = (bf16[4,12,56,128]{3,2,1,0:T(8,128)(2,1)}, bf16[4,12,56,128]{3,2,1,0:T(8,128)(2,1)S(1)}, u32[]{:S(2)}) copy-start(bf16[4,12,56,128]{3,2,1,0:T(8,128)(2,1)S(1)} %all_to_all.32) | copy-start | bytes 2064388
  90.9 14.6 %collective-permute-start.1 = (bf16[48,56,128]{2,1,0:T(8,128)(2,1)S(1)}, bf16[48,56,128]{2,1,0:T(8,128)(2,1)S(1)}, u32[]{:S(2)}, u32[]{:S(2)}) collective-permute-start(bf16[48,56,128]{2,1,0:T(8,128)(2,1)S(1)} %bitcast.16), channel_id=1, source_target_pairs={{0,8},{8,0},{1,9},{9,1},{2,10},{10,2},{3,11},{11,3},{4,12},{12,4},... | collective-permute-start | bytes 2064392 | tf_op jit(solution)/shard_map/ppermute | solution.py:163
  105.5 8.2 %copy-start.2 = (f32[32,128]{1,0:T(8,128)S(1)}, f32[32,128]{1,0:T(8,128)}, u32[]{:S(2)}) copy-start(f32[32,128]{1,0:T(8,128)} %evaluate.2) | copy-start | bytes 49156
  105.5 0.9 copy-start.1

commit v2 on v1

v2 whole, which is shorter than its diff:
```python
import jax
import jax.numpy as jnp
from jax import lax
from jax.experimental import pallas as pl
from jax.experimental.pallas import tpu as pltpu
from jax.sharding import Mesh, PartitionSpec as P

X, Z, CORES = 4, 12, 2
LMAX = 6
LM = 49
ROWS = 56
R = 128
SLOTS = 256
LANES = 128
PTS = 4096
HALF = 48
BLOCK = 24
STEPS = HALF // BLOCK
HIGH, LOW = 32, 128
TILE = 16

f32 = jnp.float32
bf16 = jnp.bfloat16


def radial_grid():
    shape = (R // TILE, TILE, SLOTS)
    grid = lax.broadcasted_iota(jnp.int32, shape, 0) * TILE + lax.broadcasted_iota(jnp.int32, shape, 1)
    return grid.astype(f32).astype(bf16)


def tile_of(row):
    return jnp.broadcast_to(row, (TILE, SLOTS)).astype(bf16)[None]


def hat_rows(grid, index, fraction):
    index = index.astype(f32)
    upper = jnp.where(grid == tile_of(index + 1.0), tile_of(fraction), jnp.zeros((), bf16))
    return jnp.where(grid == tile_of(index), tile_of(1.0 - fraction), upper).reshape(R, SLOTS)


def one_hot_low(grid, points):
    low = tile_of((points & (LOW - 1)).astype(f32))
    return jnp.where(grid == low, jnp.ones((), bf16), jnp.zeros((), bf16)).reshape(LOW, SLOTS)


def is_high(points):
    return lax.broadcasted_iota(jnp.int32, (HIGH, SLOTS), 0) == lax.shift_right_logical(points, 7)


def moments_kernel(
    half_ref,
    count_ref,
    rho_ref,
    point_hbm,
    index_hbm,
    fraction_hbm,
    angular_hbm,
    out_ref,
    point_ref,
    index_ref,
    fraction_ref,
    angular_ref,
    left_ref,
    right_ref,
    task_sems,
    angular_sems,
):
    first = pl.multiple_of(half_ref[0] * HALF, HALF)

    def task_copy(n):
        source = (point_hbm, index_hbm, fraction_hbm)[n]
        target = (point_ref, index_ref, fraction_ref)[n]
        return pltpu.make_async_copy(source.at[pl.ds(first, HALF), :], target, task_sems.at[n])

    def angular_copy(step):
        source = angular_hbm.at[:, pl.ds(first + step * BLOCK, BLOCK), :]
        return pltpu.make_async_copy(source, angular_ref.at[step], angular_sems.at[step])

    for n in range(3):
        task_copy(n).start()
    for step in range(STEPS):
        angular_copy(step).start()

    rho = rho_ref[...]
    big = rho.astype(bf16)
    small = (rho - big.astype(f32)).astype(bf16)
    rho_parts = jnp.concatenate([big, small], axis=1)
    slot = lax.broadcasted_iota(jnp.int32, (1, SLOTS), 1)
    grid = radial_grid()
    filler = jnp.zeros(((ROWS - LM) * BLOCK, LANES), f32)
    left_ref[LM * BLOCK :, :] = filler
    right_ref[LM * BLOCK :, :] = filler
    for n in range(3):
        task_copy(n).wait()

    def block(step, carry):
        base = pl.multiple_of(step * BLOCK, BLOCK)
        points = point_ref[pl.ds(base, BLOCK), :]
        index = index_ref[pl.ds(base, BLOCK), :]
        fraction = fraction_ref[pl.ds(base, BLOCK), :]
        densities = []
        for i in range(BLOCK):
            low = one_hot_low(grid, points[i : i + 1, :])
            columns = jnp.dot(rho_parts, jnp.concatenate([low, low], axis=0), preferred_element_type=f32)
            picked = jnp.sum(jnp.where(is_high(points[i : i + 1, :]), columns, 0.0), axis=0, keepdims=True)
            densities.append(jnp.where(slot < count_ref[first + base + i], picked, 0.0))
        densities = jnp.concatenate(densities, axis=0)
        pltpu.make_async_copy(
            angular_hbm.at[:, pl.ds(first + base, BLOCK), :], angular_ref.at[step], angular_sems.at[step]
        ).wait()
        for m in range(LM):
            weighted = angular_ref[step, m].astype(f32) * densities
            left_ref[m * BLOCK : (m + 1) * BLOCK, :] = weighted[:, :LANES]
            right_ref[m * BLOCK : (m + 1) * BLOCK, :] = weighted[:, LANES:]
        for i in range(BLOCK):
            of_atom = pl.ds(i, ROWS, stride=BLOCK)
            weighted = jnp.concatenate([left_ref[of_atom, :], right_ref[of_atom, :]], axis=1).astype(bf16)
            rows = hat_rows(grid, index[i : i + 1, :], fraction[i : i + 1, :])
            out_ref[base + i] = lax.dot_general(
                weighted, rows, (((1,), (1,)), ((), ())), preferred_element_type=f32
            ).astype(out_ref.dtype)
        return carry

    lax.fori_loop(0, STEPS, block, 0)


def evaluate_kernel(
    half_ref,
    count_ref,
    before_ref,
    table_ref,
    point_ref,
    index_ref,
    fraction_ref,
    angular_ref,
    out_ref,
    left_ref,
    right_ref,
):
    first = pl.multiple_of(half_ref[0] * HALF, HALF)
    slot = lax.broadcasted_iota(jnp.int32, (1, SLOTS), 1)
    grid = radial_grid()

    def block(step, total):
        base = pl.multiple_of(step * BLOCK, BLOCK)
        start = pl.multiple_of(first + base, BLOCK)
        points = point_ref[pl.ds(start, BLOCK), :]
        index = index_ref[pl.ds(start, BLOCK), :]
        fraction = fraction_ref[pl.ds(start, BLOCK), :]
        for i in range(BLOCK):
            rows = hat_rows(grid, index[i : i + 1, :], fraction[i : i + 1, :])
            radial = jnp.dot(table_ref[base + i], rows, preferred_element_type=f32)
            of_atom = pl.ds(i, ROWS, stride=BLOCK)
            left_ref[of_atom, :] = radial[:, :LANES]
            right_ref[of_atom, :] = radial[:, LANES:]
        values = []
        for n, radial_ref in enumerate((left_ref, right_ref)):
            sums = [jnp.zeros((BLOCK, LANES), f32)] * 2
            for m in range(LM):
                angular = angular_ref[m, pl.ds(start, BLOCK), n * LANES : (n + 1) * LANES].astype(f32)
                sums[m % 2] = sums[m % 2] + angular * radial_ref[m * BLOCK : (m + 1) * BLOCK, :]
            values.append(sums[0] + sums[1])
        values = jnp.concatenate(values, axis=1)
        for i in range(BLOCK):
            value = jnp.where(slot < count_ref[start + i], values[i : i + 1, :], 0.0)
            big = value.astype(bf16).astype(f32)
            small = value - big
            high = is_high(points[i : i + 1, :])
            spread = jnp.concatenate([jnp.where(high, big, 0.0), jnp.where(high, small, 0.0)], axis=0)
            low = one_hot_low(grid, points[i : i + 1, :])
            total = total + lax.dot_general(
                spread.astype(bf16), low, (((1,), (1,)), ((), ())), preferred_element_type=f32
            )
        return total

    total = lax.fori_loop(0, STEPS, block, jnp.zeros((2 * HIGH, LOW), f32))
    out_ref[...] = before_ref[...] + (total[:HIGH] + total[HIGH:])


def solve_kernel(parts_ref, green_ref, table_ref):
    moments = jnp.sum(parts_ref[...].astype(f32), axis=0)
    row = lax.broadcasted_iota(jnp.int32, (ROWS, R), 0)
    table = jnp.zeros((ROWS, R), f32)
    for degree in range(LMAX + 1):
        of_degree = (row >= degree * degree) & (row < (degree + 1) * (degree + 1))
        table = table + jnp.dot(
            jnp.where(of_degree, moments, 0.0),
            green_ref[degree],
            precision=lax.Precision.HIGHEST,
            preferred_element_type=f32,
        )
    table_ref[...] = jnp.broadcast_to(table.astype(bf16), (Z, ROWS, R))


VMEM = pl.BlockSpec(memory_space=pltpu.VMEM)
SMEM = pl.BlockSpec(memory_space=pltpu.SMEM)
ANY = pl.BlockSpec(memory_space=pl.ANY)


def moments_of(half, count, rho, points, index, fraction, angular, dtype):
    return pl.pallas_call(
        moments_kernel,
        out_shape=jax.ShapeDtypeStruct((HALF, ROWS, R), dtype),
        in_specs=[SMEM, SMEM, VMEM, ANY, ANY, ANY, ANY],
        out_specs=VMEM,
        scratch_shapes=[
            pltpu.VMEM((HALF, SLOTS), jnp.int32),
            pltpu.VMEM((HALF, SLOTS), jnp.int32),
            pltpu.VMEM((HALF, SLOTS), f32),
            pltpu.VMEM((STEPS, LM, BLOCK, SLOTS), bf16),
            pltpu.VMEM((ROWS * BLOCK, LANES), f32),
            pltpu.VMEM((ROWS * BLOCK, LANES), f32),
            pltpu.SemaphoreType.DMA((3,)),
            pltpu.SemaphoreType.DMA((STEPS,)),
        ],
        name="moments",
    )(half, count, rho, points, index, fraction, angular)


def evaluated(half, count, before, table, points, index, fraction, angular):
    return pl.pallas_call(
        evaluate_kernel,
        out_shape=jax.ShapeDtypeStruct((HIGH, LOW), f32),
        in_specs=[SMEM, SMEM] + [VMEM] * 6,
        out_specs=VMEM,
        scratch_shapes=[pltpu.VMEM((ROWS * BLOCK, LANES), f32)] * 2,
        name="evaluate",
    )(half, count, before, table, points, index, fraction, angular)


def solved(parts, green):
    return pl.pallas_call(
        solve_kernel,
        out_shape=jax.ShapeDtypeStruct((Z, ROWS, R), bf16),
        in_specs=[VMEM, VMEM],
        out_specs=VMEM,
        name="solve",
    )(parts, green)


def exchanged(array, axis):
    return lax.all_to_all(array, axis, split_axis=0, concat_axis=0, tiled=True)


def to_other_core(array):
    return lax.ppermute(array, "core", [(0, 1), (1, 0)])


def near(array):
    return pltpu.with_memory_space_constraint(array, pltpu.VMEM)


def per_device(rho, task_point, task_count, radial_index, fraction, angular, green):
    core = lax.axis_index("core")
    own = core.astype(jnp.int32).reshape(1)
    other = 1 - own
    tasks = (task_point[0], radial_index[0], fraction[0], angular[0].transpose(1, 0, 2))
    count = task_count[0]
    rho = rho.reshape(HIGH, LOW)

    sent = moments_of(other, count, rho, *tasks, bf16)
    arrived = to_other_core(sent)
    kept = moments_of(own, count, rho, *tasks, f32)
    chip = (kept + arrived.astype(f32)).astype(bf16)
    along_x = exchanged(chip.reshape(X, Z, ROWS, R), "x").astype(f32)
    plane = ((along_x[0] + along_x[1]) + (along_x[2] + along_x[3])).astype(bf16)
    column = solved(near(exchanged(plane, "z")), near(green))

    column = exchanged(column, "z")
    half = exchanged(jnp.broadcast_to(column, (X, Z, ROWS, R)), "x").reshape(HALF, ROWS, R)
    other_half = to_other_core(half)
    tasks = [near(array) for array in tasks]
    terms = evaluated(own, count, jnp.zeros((HIGH, LOW), f32), near(half), *tasks)
    terms = evaluated(other, count, terms, near(other_half), *tasks)
    return exchanged(terms.reshape(8, PTS // 8), "atom").sum(axis=0)


def solution(mesh):
    mesh = Mesh(mesh.devices.reshape(X, Z, CORES, 8), ("x", "z", "core", "atom"))
    shell = ("x", "z", "core")
    in_specs = (
        P(shell),
        P(shell, "atom", None),
        P(shell, "atom"),
        P(shell, "atom", None),
        P(shell, "atom", None),
        P(shell, "atom", None, None),
        P(),
    )
    return jax.shard_map(
        per_device, mesh=mesh, in_specs=in_specs, out_specs=P((*shell, "atom")), check_vma=False
    )
```

time: 129 us -> 116 us (0.90)
  Pallas kernels: 34.9 us -> 19.9 us
  blocking collectives: 69.2 us -> 70.5 us
    pallas_call x2, Pallas kernels: 18.1 us -> 11 us  [moments_of(): pl.pallas_call(moments_kernel, out_shape=jax.ShapeDtypeStruct((HALF, ROWS...]
    pallas_call x2, Pallas kernels: 14.6 us -> 7.7 us  [evaluated(): pl.pallas_call(evaluate_kernel, out_shape=jax.ShapeDtypeStruct((HIGH, LOW...]
    all_to_all x5, blocking collectives: 69.2 us -> 70.5 us  [exchanged(): return lax.all_to_all(array, axis, split_axis=0, concat_axis=0, tiled=True)]
  transfers between devices with their start and end apart: 2 -> 2, of which waited for: 0 -> 0; matrix products, arithmetic and copies ran while one was open for 0% -> 1% of each run, Pallas kernels for 13% -> 8%
where the time goes in v2:
time: 116 us; the launch traced here: 115 us
  blocking collectives  70.5 us (61%)
  Pallas kernels  19.9 us (17%)
  starting transfers between devices  19.6 us (17%)
  local copies, waits for them, and re-layouts  2.49 us (2%)
  other arithmetic  2.24 us (2%)
    all_to_all x5, blocking collectives, exchanged(): return lax.all_to_all(array, axis, split_axis=0, concat_axis=0, tiled=True)  70.5 us
    ppermute x2, starting transfers between devices, to_other_core(): return lax.ppermute(array, 'core', [(0, 1), (1, 0)])  19.6 us
    pallas_call x2, Pallas kernels, moments_of(): pl.pallas_call(moments_kernel, out_shape=jax.ShapeDtypeStruct((HALF, ROWS...  11 us
    pallas_call x2, Pallas kernels, evaluated(): pl.pallas_call(evaluate_kernel, out_shape=jax.ShapeDtypeStruct((HIGH, LOW...  7.7 us
  transfers between devices with their start and end apart: 2, of which 0 were waited for; matrix products, arithmetic and copies ran while one was open for 1% of the time, Pallas kernels for 8%

profile of v2, /device:TPU:1, one launch (start us, length us, event | category | flops | bytes accessed | tf_op | source)
XLA Modules:
  0.0 114.8 jit_solution(4014950890937515023)
XLA Ops:
  0.0 5.4 %moments.3 = bf16[48,56,128]{2,1,0:T(8,128)(2,1)} custom-call(s32[1]{0:T(128)S(6)} %sub.3.half_ref, s32[96]{0:T(128)} %bitcast.34, f32[32,128]{1,0:T(8,128)} %bitcast.31, s32[96,256]{1,0:T(8,128)} %bitcast.18, s32[96,256]{1,0:T(8,128)} %bitcast.22, f32[96,256]{1,0:T(8,128)} %bitcast.26, bf16[49,96,256]{2,1,0:T(8,128)(2,1)} %bitcast.14), custom_call_target="tpu_custom_call" | custom-call | tf_op jit(solution)/shard_map/moments/pallas_call | solution.py:202
  5.4 12.4 %collective-permute-start = (bf16[48,56,128]{2,1,0:T(8,128)(2,1)}, bf16[48,56,128]{2,1,0:T(8,128)(2,1)S(1)}, u32[]{:S(2)}, u32[]{:S(2)}) collective-permute-start(bf16[48,56,128]{2,1,0:T(8,128)(2,1)} %moments.3), channel_id=1, source_target_pairs={{0,8},{8,0},{1,9},{9,1},{2,10},{10,2},{3,11},{11,3},{4,12},{12,4},... | collective-permute-start | bytes 2064392 | tf_op jit(solution)/shard_map/ppermute | solution.py:247
  17.8 5.6 %moments.2 = f32[48,56,128]{2,1,0:T(8,128)} custom-call(s32[1]{0:T(128)} %bitcast.half_ref, s32[96]{0:T(128)} %bitcast.35, f32[32,128]{1,0:T(8,128)} %bitcast.32, s32[96,256]{1,0:T(8,128)} %bitcast.19, s32[96,256]{1,0:T(8,128)} %bitcast.23, f32[96,256]{1,0:T(8,128)} %bitcast.27, bf16[49,96,256]{2,1,0:T(8,128)(2,1)} %bitcast.15), custom_call_target="tpu_custom_call" | custom-call | tf_op jit(solution)/shard_map/moments/pallas_call | solution.py:202
  23.4 0.0 collective-permute-done
  23.4 1.5 %add_convert_fusion = bf16[48,56,128]{2,1,0:T(8,128)(2,1)S(1)} fusion(f32[48,56,128]{2,1,0:T(8,128)} %moments.2, bf16[48,56,128]{2,1,0:T(8,128)(2,1)S(1)} %collective-permute-done), kind=kLoop, calls=%fused_computation | loop fusion | flops 1032192 | bytes 2752512 | tf_op jit(solution)/shard_map/convert_element_type | solution.py:265
  24.9 13.7 %all_to_all.29 = bf16[4,12,56,128]{3,2,1,0:T(8,128)(2,1)S(1)} all-to-all(bf16[4,12,56,128]{3,2,1,0:T(8,128)(2,1)S(1)} %bitcast.30), channel_id=1, replica_groups=mesh['x'=4,'z'=12,'core'=2,'atom'=8] {'x'}, dimensions={0} | all-to-all | bytes 1376256 | tf_op jit(solution)/shard_map/all_to_all | solution.py:243
  38.6 0.1 convert_element_type.17
  38.7 0.0 copy-start.4
  38.7 0.1 fusion.2
  38.8 17.5 %all_to_all.30.parts_ref = bf16[12,56,128]{2,1,0:T(8,128)(2,1)S(1)} all-to-all(bf16[12,56,128]{2,1,0:T(8,128)(2,1)S(1)} %fusion.2), channel_id=1, replica_groups=mesh['x'=4,'z'=12,'core'=2,'atom'=8] {'z'}, dimensions={0} | all-to-all | bytes 344064 | tf_op jit(solution)/shard_map/all_to_all | solution.py:243
  56.3 0.0 copy-done.4
  56.3 1.2 %solve.1 = bf16[12,56,128]{2,1,0:T(8,128)(2,1)} custom-call(bf16[12,56,128]{2,1,0:T(8,128)(2,1)S(1)} %all_to_all.30.parts_ref, f32[7,128,128]{2,1,0:T(8,128)S(1)} %copy-done.4), custom_call_target="tpu_custom_call" | custom-call | tf_op jit(solution)/shard_map/solve/pallas_call | solution.py:233
  57.5 0.0 copy-start
  57.5 0.0 copy-start.1
  57.5 14.9 %all_to_all.31 = bf16[12,56,128]{2,1,0:T(8,128)(2,1)S(1)} all-to-all(bf16[12,56,128]{2,1,0:T(8,128)(2,1)} %solve.1), channel_id=1, replica_groups=mesh['x'=4,'z'=12,'core'=2,'atom'=8] {'z'}, dimensions={0} | all-to-all | bytes 344064 | tf_op jit(solution)/shard_map/all_to_all | solution.py:243
  72.4 0.1 broadcast_in_dim.7
  72.5 10.9 %all_to_all.32 = bf16[4,12,56,128]{3,2,1,0:T(8,128)(2,1)} all-to-all(bf16[4,12,56,128]{3,2,1,0:T(8,128)(2,1)S(1)} %broadcast_in_dim.7), channel_id=1, replica_groups=mesh['x'=4,'z'=12,'core'=2,'atom'=8] {'x'}, dimensions={0} | all-to-all | bytes 1376256 | tf_op jit(solution)/shard_map/all_to_all | solution.py:243
  83.4 7.2 %collective-permute-start.1 = (bf16[48,56,128]{2,1,0:T(8,128)(2,1)}, bf16[48,56,128]{2,1,0:T(8,128)(2,1)}, u32[]{:S(2)}, u32[]{:S(2)}) collective-permute-start(bf16[48,56,128]{2,1,0:T(8,128)(2,1)} %bitcast.11.table_ref), channel_id=1, source_target_pairs={{0,8},{8,0},{1,9},{9,1},{2,10},{10,2},{3,11},{11,3},{4,12},{12,4},... | collective-permute-start | bytes 2064392 | tf_op jit(solution)/shard_map/ppermute | solution.py:247
  90.7 0.6 broadcast_in_dim.6.before_ref
  91.3 0.0 copy-done
  91.3 0.0 copy-done.1
  91.3 0.0 copy-start.2
  91.3 0.9 copy-done.2
  92.2 0.0 copy-start.3
  92.2 0.9 copy-done.3
  93.1 3.9 %evaluate.2.before_ref = f32[32,128]{1,0:T(8,128)} custom-call(s32[1]{0:T(128)} %bitcast.half_ref, s32[96]{0:T(128)} %bitcast.36, f32[32,128]{1,0:T(8,128)} %broadcast_in_dim.6.before_ref, bf16[48,56,128]{2,1,0:T(8,128)(2,1)} %bitcast.11.table_ref, s32[96,256]{1,0:T(8,128)S(1)} %bitcast.20, s32[96,256]{1,0:T(8,128)S(1)} %bitcast.24, f32[96,256]{1,0:T(8,128)S(1)} %bitcast.28, ...), custom_call_target="tpu_custom_call" | custom-call | tf_op jit(solution)/shard_map/evaluate/pallas_call | solution.py:222
  96.9 0.0 collective-permute-done.1.table_ref
  96.9 3.8 %evaluate.3 = f32[32,128]{1,0:T(8,128)} custom-call(s32[1]{0:T(128)S(6)} %sub.3.half_ref, s32[96]{0:T(128)} %bitcast.37, f32[32,128]{1,0:T(8,128)} %evaluate.2.before_ref, bf16[48,56,128]{2,1,0:T(8,128)(2,1)} %collective-permute-done.1.table_ref, s32[96,256]{1,0:T(8,128)S(1)} %bitcast.21, s32[96,256]{1,0:T(8,128)S(1)} %bitcast.25, f32[96,256]{1,0:T(8,128)S(1)} %bitcast.29, ...), custom_call_target="tpu_custom_call" | custom-call | tf_op jit(solution)/shard_map/evaluate/pallas_call | solution.py:222
  100.8 13.4 %all_to_all.33 = f32[8,1,512]{2,1,0:T(1,128)S(1)} all-to-all(f32[8,1,512]{2,1,0:T(1,128)} %bitcast.33), channel_id=1, replica_groups=mesh['x'=4,'z'=12,'core'=2,'atom'=8] {'atom'}, dimensions={0} | all-to-all | bytes 32768 | tf_op jit(solution)/shard_map/all_to_all | solution.py:243
  114.2 0.6 reduce_sum.9
Async XLA Ops:
  5.4 18.0 %collective-permute-start = (bf16[48,56,128]{2,1,0:T(8,128)(2,1)}, bf16[48,56,128]{2,1,0:T(8,128)(2,1)S(1)}, u32[]{:S(2)}, u32[]{:S(2)}) collective-permute-start(bf16[48,56,128]{2,1,0:T(8,128)(2,1)} %moments.3), channel_id=1, source_target_pairs={{0,8},{8,0},{1,9},{9,1},{2,10},{10,2},{3,11},{11,3},{4,12},{12,4},... | collective-permute-start | bytes 2064392 | tf_op jit(solution)/shard_map/ppermute | solution.py:247
  38.7 17.6 %copy-start.4 = (f32[7,128,128]{2,1,0:T(8,128)S(1)}, f32[7,128,128]{2,1,0:T(8,128)}, u32[]{:S(2)}) copy-start(f32[7,128,128]{2,1,0:T(8,128)} %green_ref.1) | copy-start | bytes 1376260
  57.5 33.8 %copy-start = (bf16[1,96,49,256]{3,1,2,0:T(8,128)(2,1)S(1)}, bf16[1,96,49,256]{3,1,2,0:T(8,128)(2,1)}, u32[]{:S(2)}) copy-start(bf16[1,96,49,256]{3,1,2,0:T(8,128)(2,1)} %param.12) | copy-start | bytes 7225348
  57.5 33.8 %copy-start.1 = (s32[1,96,256]{2,1,0:T(8,128)S(1)}, s32[1,96,256]{2,1,0:T(8,128)}, u32[]{:S(2)}) copy-start(s32[1,96,256]{2,1,0:T(8,128)} %param.8) | copy-start | bytes 294916
  83.4 13.5 %collective-permute-start.1 = (bf16[48,56,128]{2,1,0:T(8,128)(2,1)}, bf16[48,56,128]{2,1,0:T(8,128)(2,1)}, u32[]{:S(2)}, u32[]{:S(2)}) collective-permute-start(bf16[48,56,128]{2,1,0:T(8,128)(2,1)} %bitcast.11.table_ref), channel_id=1, source_target_pairs={{0,8},{8,0},{1,9},{9,1},{2,10},{10,2},{3,11},{11,3},{4,12},{12,4},... | collective-permute-start | bytes 2064392 | tf_op jit(solution)/shard_map/ppermute | solution.py:247
  91.3 0.9 copy-start.2
  92.2 0.9 copy-start.3

commit v3 on v2

--- a/solution.py
+++ b/solution.py
@@ -48,15 +48,51 @@
     return lax.broadcasted_iota(jnp.int32, (HIGH, SLOTS), 0) == lax.shift_right_logical(points, 7)
 
 
-def moments_kernel(
+def add_moments(base, counts, tasks, angular_rows, rho_ref, out_ref, left_ref, right_ref):
+    points, index, fraction = tasks
+    rho = rho_ref[...]
+    big = rho.astype(bf16)
+    small = (rho - big.astype(f32)).astype(bf16)
+    rho_parts = jnp.concatenate([big, small], axis=1)
+    slot = lax.broadcasted_iota(jnp.int32, (1, SLOTS), 1)
+    grid = radial_grid()
+    densities = []
+    for i in range(BLOCK):
+        low = one_hot_low(grid, points[i : i + 1, :])
+        columns = jnp.dot(rho_parts, jnp.concatenate([low, low], axis=0), preferred_element_type=f32)
+        picked = jnp.sum(jnp.where(is_high(points[i : i + 1, :]), columns, 0.0), axis=0, keepdims=True)
+        densities.append(jnp.where(slot < counts(i), picked, 0.0))
+    densities = jnp.concatenate(densities, axis=0)
+    for m, angular in enumerate(angular_rows()):
+        weighted = angular.astype(f32) * densities
+        left_ref[m * BLOCK : (m + 1) * BLOCK, :] = weighted[:, :LANES]
+        right_ref[m * BLOCK : (m + 1) * BLOCK, :] = weighted[:, LANES:]
+    for i in range(BLOCK):
+        of_atom = pl.ds(i, ROWS, stride=BLOCK)
+        weighted = jnp.concatenate([left_ref[of_atom, :], right_ref[of_atom, :]], axis=1).astype(bf16)
+        rows = hat_rows(grid, index[i : i + 1, :], fraction[i : i + 1, :])
+        out_ref[base + i] = lax.dot_general(
+            weighted, rows, (((1,), (1,)), ((), ())), preferred_element_type=f32
+        ).astype(out_ref.dtype)
+
+
+def fill(left_ref, right_ref):
+    filler = jnp.zeros(((ROWS - LM) * BLOCK, LANES), f32)
+    left_ref[LM * BLOCK :, :] = filler
+    right_ref[LM * BLOCK :, :] = filler
+
+
+def first_moments_kernel(
     half_ref,
-    count_ref,
-    rho_ref,
+    count_hbm,
+    rho_hbm,
     point_hbm,
     index_hbm,
     fraction_hbm,
     angular_hbm,
     out_ref,
+    count_ref,
+    rho_ref,
     point_ref,
     index_ref,
     fraction_ref,
@@ -67,77 +103,79 @@
     angular_sems,
 ):
     first = pl.multiple_of(half_ref[0] * HALF, HALF)
+    task_refs = (point_ref, index_ref, fraction_ref)
 
     def task_copy(n):
         source = (point_hbm, index_hbm, fraction_hbm)[n]
-        target = (point_ref, index_ref, fraction_ref)[n]
-        return pltpu.make_async_copy(source.at[pl.ds(first, HALF), :], target, task_sems.at[n])
+        return pltpu.make_async_copy(source.at[pl.ds(first, HALF), :], task_refs[n], task_sems.at[n])
+
+    def rho_copy():
+        return pltpu.make_async_copy(rho_hbm, rho_ref, task_sems.at[3])
+
+    def count_copy():
+        return pltpu.make_async_copy(count_hbm, count_ref, task_sems.at[4])
 
     def angular_copy(step):
         source = angular_hbm.at[:, pl.ds(first + step * BLOCK, BLOCK), :]
         return pltpu.make_async_copy(source, angular_ref.at[step], angular_sems.at[step])
 
+    rho_copy().start()
+    count_copy().start()
     for n in range(3):
         task_copy(n).start()
     for step in range(STEPS):
         angular_copy(step).start()
-
-    rho = rho_ref[...]
-    big = rho.astype(bf16)
-    small = (rho - big.astype(f32)).astype(bf16)
-    rho_parts = jnp.concatenate([big, small], axis=1)
-    slot = lax.broadcasted_iota(jnp.int32, (1, SLOTS), 1)
-    grid = radial_grid()
-    filler = jnp.zeros(((ROWS - LM) * BLOCK, LANES), f32)
-    left_ref[LM * BLOCK :, :] = filler
-    right_ref[LM * BLOCK :, :] = filler
+    fill(left_ref, right_ref)
+    rho_copy().wait()
+    count_copy().wait()
     for n in range(3):
         task_copy(n).wait()
 
     def block(step, carry):
         base = pl.multiple_of(step * BLOCK, BLOCK)
-        points = point_ref[pl.ds(base, BLOCK), :]
-        index = index_ref[pl.ds(base, BLOCK), :]
-        fraction = fraction_ref[pl.ds(base, BLOCK), :]
-        densities = []
-        for i in range(BLOCK):
-            low = one_hot_low(grid, points[i : i + 1, :])
-            columns = jnp.dot(rho_parts, jnp.concatenate([low, low], axis=0), preferred_element_type=f32)
-            picked = jnp.sum(jnp.where(is_high(points[i : i + 1, :]), columns, 0.0), axis=0, keepdims=True)
-            densities.append(jnp.where(slot < count_ref[first + base + i], picked, 0.0))
-        densities = jnp.concatenate(densities, axis=0)
-        pltpu.make_async_copy(
-            angular_hbm.at[:, pl.ds(first + base, BLOCK), :], angular_ref.at[step], angular_sems.at[step]
-        ).wait()
-        for m in range(LM):
-            weighted = angular_ref[step, m].astype(f32) * densities
-            left_ref[m * BLOCK : (m + 1) * BLOCK, :] = weighted[:, :LANES]
-            right_ref[m * BLOCK : (m + 1) * BLOCK, :] = weighted[:, LANES:]
-        for i in range(BLOCK):
-            of_atom = pl.ds(i, ROWS, stride=BLOCK)
-            weighted = jnp.concatenate([left_ref[of_atom, :], right_ref[of_atom, :]], axis=1).astype(bf16)
-            rows = hat_rows(grid, index[i : i + 1, :], fraction[i : i + 1, :])
-            out_ref[base + i] = lax.dot_general(
-                weighted, rows, (((1,), (1,)), ((), ())), preferred_element_type=f32
-            ).astype(out_ref.dtype)
+
+        def angular_rows():
+            angular_copy(step).wait()
+            return (angular_ref[step, m] for m in range(LM))
+
+        tasks = [ref[pl.ds(base, BLOCK), :] for ref in task_refs]
+        add_moments(
+            base, lambda i: count_ref[0, first + base + i], tasks, angular_rows, rho_ref, out_ref, left_ref, right_ref
+        )
         return carry
 
     lax.fori_loop(0, STEPS, block, 0)
 
 
+def moments_kernel(
+    half_ref, count_ref, rho_ref, point_ref, index_ref, fraction_ref, angular_ref, out_ref, left_ref, right_ref
+):
+    first = pl.multiple_of(half_ref[0] * HALF, HALF)
+    fill(left_ref, right_ref)
+
+    def block(step, carry):
+        base = pl.multiple_of(step * BLOCK, BLOCK)
+        start = pl.multiple_of(first + base, BLOCK)
+        tasks = [ref[pl.ds(start, BLOCK), :] for ref in (point_ref, index_ref, fraction_ref)]
+        add_moments(
+            base,
+            lambda i: count_ref[0, start + i],
+            tasks,
+            lambda: (angular_ref[m, pl.ds(start, BLOCK), :] for m in range(LM)),
+            rho_ref,
+            out_ref,
+            left_ref,
+            right_ref,
+        )
+        return carry
+
+    lax.fori_loop(0, STEPS, block, 0)
+
+
 def evaluate_kernel(
-    half_ref,
-    count_ref,
-    before_ref,
-    table_ref,
-    point_ref,
-    index_ref,
-    fraction_ref,
-    angular_ref,
-    out_ref,
-    left_ref,
-    right_ref,
+    half_ref, count_ref, table_ref, point_ref, index_ref, fraction_ref, angular_ref, *refs
 ):
+    *before_ref, out_ref, left_ref, right_ref = refs
     first = pl.multiple_of(half_ref[0] * HALF, HALF)
     slot = lax.broadcasted_iota(jnp.int32, (1, SLOTS), 1)
     grid = radial_grid()
@@ -163,7 +201,7 @@
             values.append(sums[0] + sums[1])
         values = jnp.concatenate(values, axis=1)
         for i in range(BLOCK):
-            value = jnp.where(slot < count_ref[start + i], values[i : i + 1, :], 0.0)
+            value = jnp.where(slot < count_ref[0, start + i], values[i : i + 1, :], 0.0)
             big = value.astype(bf16).astype(f32)
             small = value - big
             high = is_high(points[i : i + 1, :])
@@ -175,7 +213,8 @@
         return total
 
     total = lax.fori_loop(0, STEPS, block, jnp.zeros((2 * HIGH, LOW), f32))
-    out_ref[...] = before_ref[...] + (total[:HIGH] + total[HIGH:])
+    total = total[:HIGH] + total[HIGH:]
+    out_ref[...] = total + before_ref[0][...] if before_ref else total
 
 
 def solve_kernel(parts_ref, green_ref, table_ref):
@@ -195,46 +234,64 @@
 
 VMEM = pl.BlockSpec(memory_space=pltpu.VMEM)
 SMEM = pl.BlockSpec(memory_space=pltpu.SMEM)
-ANY = pl.BlockSpec(memory_space=pl.ANY)
-
-
-def moments_of(half, count, rho, points, index, fraction, angular, dtype):
+HBM = pl.BlockSpec(memory_space=pltpu.HBM)
+GRANT = pltpu.CompilerParams(vmem_limit_bytes=16 << 20)
+
+
+def first_moments_of(half, count, rho, points, index, fraction, angular):
     return pl.pallas_call(
-        moments_kernel,
-        out_shape=jax.ShapeDtypeStruct((HALF, ROWS, R), dtype),
-        in_specs=[SMEM, SMEM, VMEM, ANY, ANY, ANY, ANY],
+        first_moments_kernel,
+        out_shape=pltpu.VMEM((HALF, ROWS, R), bf16),
+        in_specs=[SMEM] + [HBM] * 6,
         out_specs=VMEM,
         scratch_shapes=[
+            pltpu.SMEM((1, 2 * HALF), jnp.int32),
+            pltpu.VMEM((HIGH, LOW), f32),
             pltpu.VMEM((HALF, SLOTS), jnp.int32),
             pltpu.VMEM((HALF, SLOTS), jnp.int32),
             pltpu.VMEM((HALF, SLOTS), f32),
             pltpu.VMEM((STEPS, LM, BLOCK, SLOTS), bf16),
             pltpu.VMEM((ROWS * BLOCK, LANES), f32),
             pltpu.VMEM((ROWS * BLOCK, LANES), f32),
-            pltpu.SemaphoreType.DMA((3,)),
+            pltpu.SemaphoreType.DMA((5,)),
             pltpu.SemaphoreType.DMA((STEPS,)),
         ],
+        compiler_params=GRANT,
+        name="first_moments",
+    )(half, count, rho, points, index, fraction, angular)
+
+
+def moments_of(half, count, rho, points, index, fraction, angular):
+    return pl.pallas_call(
+        moments_kernel,
+        out_shape=pltpu.VMEM((HALF, ROWS, R), f32),
+        in_specs=[SMEM, SMEM] + [VMEM] * 5,
+        out_specs=VMEM,
+        scratch_shapes=[pltpu.VMEM((ROWS * BLOCK, LANES), f32)] * 2,
+        compiler_params=GRANT,
         name="moments",
     )(half, count, rho, points, index, fraction, angular)
 
 
-def evaluated(half, count, before, table, points, index, fraction, angular):
+def evaluated(half, count, table, points, index, fraction, angular, *before):
     return pl.pallas_call(
         evaluate_kernel,
-        out_shape=jax.ShapeDtypeStruct((HIGH, LOW), f32),
-        in_specs=[SMEM, SMEM] + [VMEM] * 6,
+        out_shape=pltpu.VMEM((HIGH, LOW), f32),
+        in_specs=[SMEM, SMEM] + [VMEM] * (5 + len(before)),
         out_specs=VMEM,
         scratch_shapes=[pltpu.VMEM((ROWS * BLOCK, LANES), f32)] * 2,
+        compiler_params=GRANT,
         name="evaluate",
-    )(half, count, before, table, points, index, fraction, angular)
+    )(half, count, table, points, index, fraction, angular, *before)
 
 
 def solved(parts, green):
     return pl.pallas_call(
         solve_kernel,
-        out_shape=jax.ShapeDtypeStruct((Z, ROWS, R), bf16),
+        out_shape=pltpu.VMEM((Z, ROWS, R), bf16),
         in_specs=[VMEM, VMEM],
         out_specs=VMEM,
+        compiler_params=GRANT,
         name="solve",
     )(parts, green)
 
@@ -245,6 +302,10 @@
 
 def to_other_core(array):
     return lax.ppermute(array, "core", [(0, 1), (1, 0)])
+
+
+def far(array):
+    return pltpu.with_memory_space_constraint(array, pltpu.HBM)
 
 
 def near(array):
@@ -256,12 +317,13 @@
     own = core.astype(jnp.int32).reshape(1)
     other = 1 - own
     tasks = (task_point[0], radial_index[0], fraction[0], angular[0].transpose(1, 0, 2))
-    count = task_count[0]
+    count = task_count
     rho = rho.reshape(HIGH, LOW)
 
-    sent = moments_of(other, count, rho, *tasks, bf16)
+    sent = first_moments_of(other, *(far(array) for array in (count, rho, *tasks)))
     arrived = to_other_core(sent)
-    kept = moments_of(own, count, rho, *tasks, f32)
+    tasks = [near(array) for array in tasks]
+    kept = moments_of(own, count, near(rho), *tasks)
     chip = (kept + arrived.astype(f32)).astype(bf16)
     along_x = exchanged(chip.reshape(X, Z, ROWS, R), "x").astype(f32)
     plane = ((along_x[0] + along_x[1]) + (along_x[2] + along_x[3])).astype(bf16)
@@ -270,9 +332,8 @@
     column = exchanged(column, "z")
     half = exchanged(jnp.broadcast_to(column, (X, Z, ROWS, R)), "x").reshape(HALF, ROWS, R)
     other_half = to_other_core(half)
-    tasks = [near(array) for array in tasks]
-    terms = evaluated(own, count, jnp.zeros((HIGH, LOW), f32), near(half), *tasks)
-    terms = evaluated(other, count, terms, near(other_half), *tasks)
+    terms = evaluated(own, count, near(half), *tasks)
+    terms = evaluated(other, count, near(other_half), *tasks, terms)
     return exchanged(terms.reshape(8, PTS // 8), "atom").sum(axis=0)
 
 

time: 116 us -> 103 us (0.89); the launches traced: 115 us -> 103 us
  Pallas kernels: 19.9 us -> 12.9 us
  local copies, waits for them, and re-layouts: 2.49 us -> 0.12 us
  other arithmetic: 2.24 us -> 0.93 us
  blocking collectives: 70.5 us -> 69.2 us
    pallas_call x5, Pallas kernels: 19.9 us -> 12.9 us  [the longest x2 5.34 us: evaluated(): pl.pallas_call(evaluate_kernel, out_shape=pltpu.VMEM((HIGH, LOW), f32), i...]
    unnamed x10 -> x14, local copies, waits for them, and re-layouts: 1.8 us -> 0.03 us
    convert_element_type x1, other arithmetic: 1.48 us -> 0.17 us  [per_device(): chip = (kept + arrived.astype(f32)).astype(bf16)]
    all_to_all x5, blocking collectives: 70.5 us -> 69.2 us  [exchanged(): return lax.all_to_all(array, axis, split_axis=0, concat_axis=0, tiled=True)]
  transfers between devices with their start and end apart: 2 -> 2, of which waited for: 0 -> 0; matrix products, arithmetic and copies ran while one was open for 1% -> 0% of each run, Pallas kernels for 8% -> 6%
where the time goes in v3:
time: 103 us
  blocking collectives  69.2 us (67%)
  starting transfers between devices  19.6 us (19%)
  Pallas kernels  12.9 us (13%)
    all_to_all x5, blocking collectives, exchanged(): return lax.all_to_all(array, axis, split_axis=0, concat_axis=0, tiled=True)  69.2 us
    ppermute x2, starting transfers between devices, to_other_core(): return lax.ppermute(array, 'core', [(0, 1), (1, 0)])  19.6 us
    pallas_call x2, Pallas kernels, evaluated(): pl.pallas_call(evaluate_kernel, out_shape=pltpu.VMEM((HIGH, LOW), f32), i...  5.34 us
    pallas_call x1, Pallas kernels, first_moments_of(): pl.pallas_call(first_moments_kernel, out_shape=pltpu.VMEM((HALF, ROWS, R)...  3.95 us
    pallas_call x1, Pallas kernels, moments_of(): pl.pallas_call(moments_kernel, out_shape=pltpu.VMEM((HALF, ROWS, R), f32)...  3.13 us
  transfers between devices with their start and end apart: 2, of which 0 were waited for; matrix products, arithmetic and copies ran while one was open for 0% of the time, Pallas kernels for 6%

profile of v3, /device:TPU:1, one launch (start us, length us, event | category | flops | bytes accessed | tf_op | source)
XLA Modules:
  0.0 103.0 jit_solution(2741586042818410316)
XLA Ops:
  0.0 0.0 copy-start
  0.0 0.0 copy-start.1
  0.0 0.0 copy-start.3
  0.0 0.0 copy-start.5
  0.0 0.0 copy-start.6
  0.0 3.9 %first_moments.1 = bf16[48,56,128]{2,1,0:T(8,128)(2,1)S(1)} custom-call(s32[1]{0:T(128)S(6)} %sub.3.half_ref, s32[1,96]{1,0:T(1,128)} %count_ref.5, f32[32,128]{1,0:T(8,128)} %bitcast.31, s32[96,256]{1,0:T(8,128)} %bitcast.19, s32[96,256]{1,0:T(8,128)} %bitcast.23, f32[96,256]{1,0:T(8,128)} %bitcast.27, bf16[49,96,256]{2,1,0:T(8,128)(2,1)} %bitcast.13), custom_call_target="tpu_custom_call" | custom-call | tf_op jit(solution)/shard_map/first_moments/pallas_call | solution.py:242
  4.0 12.4 %collective-permute-start = (bf16[48,56,128]{2,1,0:T(8,128)(2,1)S(1)}, bf16[48,56,128]{2,1,0:T(8,128)(2,1)S(1)}, u32[]{:S(2)}, u32[]{:S(2)}) collective-permute-start(bf16[48,56,128]{2,1,0:T(8,128)(2,1)S(1)} %first_moments.1), channel_id=1, source_target_pairs={{0,8},{8,0},{1,9},{9,1},{2,10},{10,2},{3,11},{11,3},{4,12},{12,4},... | collective-permute-start | bytes 2064392 | tf_op jit(solution)/shard_map/ppermute | solution.py:304
  16.4 0.0 copy-done
  16.4 0.0 copy-done.1
  16.4 0.0 copy-done.2
  16.4 0.0 copy-done.3
  16.4 0.0 copy-done.5
  16.4 0.0 copy-done.6
  16.5 3.1 %moments.1 = f32[48,56,128]{2,1,0:T(8,128)S(1)} custom-call(s32[1]{0:T(128)} %bitcast.half_ref, s32[1,96]{1,0:T(1,128)S(1)} %copy-done.6, f32[32,128]{1,0:T(8,128)S(1)} %bitcast.32, s32[96,256]{1,0:T(8,128)S(1)} %bitcast.20, s32[96,256]{1,0:T(8,128)S(1)} %bitcast.24, f32[96,256]{1,0:T(8,128)S(1)} %bitcast.28, bf16[49,96,256]{2,1,0:T(8,128)(2,1)S(1)} %bitcast.14), custom_call_target="tpu_custom_call" | custom-call | tf_op jit(solution)/shard_map/moments/pallas_call | solution.py:265
  19.6 0.0 collective-permute-done
  19.6 0.2 add_convert_fusion
  19.8 13.7 %all_to_all.29 = bf16[4,12,56,128]{3,2,1,0:T(8,128)(2,1)S(1)} all-to-all(bf16[4,12,56,128]{3,2,1,0:T(8,128)(2,1)S(1)} %bitcast.34), channel_id=1, replica_groups=mesh['x'=4,'z'=12,'core'=2,'atom'=8] {'x'}, dimensions={0} | all-to-all | bytes 1376256 | tf_op jit(solution)/shard_map/all_to_all | solution.py:300
  33.5 0.1 convert_element_type.17
  33.6 0.0 copy-start.4
  33.6 0.1 fusion.2
  33.6 17.5 %all_to_all.30.parts_ref = bf16[12,56,128]{2,1,0:T(8,128)(2,1)S(1)} all-to-all(bf16[12,56,128]{2,1,0:T(8,128)(2,1)S(1)} %fusion.2), channel_id=1, replica_groups=mesh['x'=4,'z'=12,'core'=2,'atom'=8] {'z'}, dimensions={0} | all-to-all | bytes 344064 | tf_op jit(solution)/shard_map/all_to_all | solution.py:300
  51.2 0.0 copy-done.4
  51.2 0.5 solve.1
  51.7 14.6 %all_to_all.31 = bf16[12,56,128]{2,1,0:T(8,128)(2,1)S(1)} all-to-all(bf16[12,56,128]{2,1,0:T(8,128)(2,1)S(1)} %solve.1), channel_id=1, replica_groups=mesh['x'=4,'z'=12,'core'=2,'atom'=8] {'z'}, dimensions={0} | all-to-all | bytes 344064 | tf_op jit(solution)/shard_map/all_to_all | solution.py:300
  66.3 0.1 broadcast_in_dim.3
  66.4 10.2 %all_to_all.32 = bf16[4,12,56,128]{3,2,1,0:T(8,128)(2,1)S(1)} all-to-all(bf16[4,12,56,128]{3,2,1,0:T(8,128)(2,1)S(1)} %broadcast_in_dim.3), channel_id=1, replica_groups=mesh['x'=4,'z'=12,'core'=2,'atom'=8] {'x'}, dimensions={0} | all-to-all | bytes 1376256 | tf_op jit(solution)/shard_map/all_to_all | solution.py:300
  76.6 7.2 %collective-permute-start.1 = (bf16[48,56,128]{2,1,0:T(8,128)(2,1)S(1)}, bf16[48,56,128]{2,1,0:T(8,128)(2,1)S(1)}, u32[]{:S(2)}, u32[]{:S(2)}) collective-permute-start(bf16[48,56,128]{2,1,0:T(8,128)(2,1)S(1)} %bitcast.17), channel_id=1, source_target_pairs={{0,8},{8,0},{1,9},{9,1},{2,10},{10,2},{3,11},{11,3},{4,12},{12,4},... | collective-permute-start | bytes 2064392 | tf_op jit(solution)/shard_map/ppermute | solution.py:304
  83.8 2.7 %evaluate.2.refs_0_ = f32[32,128]{1,0:T(8,128)S(1)} custom-call(s32[1]{0:T(128)} %bitcast.half_ref, s32[1,96]{1,0:T(1,128)S(1)} %copy-done.6, bf16[48,56,128]{2,1,0:T(8,128)(2,1)S(1)} %bitcast.18, s32[96,256]{1,0:T(8,128)S(1)} %bitcast.21, s32[96,256]{1,0:T(8,128)S(1)} %bitcast.25, f32[96,256]{1,0:T(8,128)S(1)} %bitcast.29, bf16[49,96,256]{2,1,0:T(8,128)(2,1)S(1)} %bitcast.15), custom_call_target="tpu_custom_call" | custom-call | tf_op jit(solution)/shard_map/evaluate/pallas_call | solution.py:277
  86.5 0.0 collective-permute-done.1.table_ref
  86.5 2.7 %evaluate.3 = f32[32,128]{1,0:T(8,128)S(1)} custom-call(s32[1]{0:T(128)S(6)} %sub.3.half_ref, s32[1,96]{1,0:T(1,128)S(1)} %copy-done.6, bf16[48,56,128]{2,1,0:T(8,128)(2,1)S(1)} %collective-permute-done.1.table_ref, s32[96,256]{1,0:T(8,128)S(1)} %bitcast.22, s32[96,256]{1,0:T(8,128)S(1)} %bitcast.26, f32[96,256]{1,0:T(8,128)S(1)} %bitcast.30, ...), custom_call_target="tpu_custom_call" | custom-call | tf_op jit(solution)/shard_map/evaluate/pallas_call | solution.py:277
  89.2 13.2 %all_to_all.33 = f32[8,1,512]{2,1,0:T(1,128)S(1)} all-to-all(f32[8,1,512]{2,1,0:T(1,128)S(1)} %bitcast.33), channel_id=1, replica_groups=mesh['x'=4,'z'=12,'core'=2,'atom'=8] {'atom'}, dimensions={0} | all-to-all | bytes 32768 | tf_op jit(solution)/shard_map/all_to_all | solution.py:300
  102.4 0.6 reduce_sum.9
  (1 shorter events, 0.0 us)
Async XLA Ops:
  0.0 16.4 %copy-start = (bf16[1,96,49,256]{3,1,2,0:T(8,128)(2,1)S(1)}, bf16[1,96,49,256]{3,1,2,0:T(8,128)(2,1)}, u32[]{:S(2)}) copy-start(bf16[1,96,49,256]{3,1,2,0:T(8,128)(2,1)} %param.12) | copy-start | bytes 7225348
  0.0 16.4 %copy-start.1 = (s32[1,96,256]{2,1,0:T(8,128)S(1)}, s32[1,96,256]{2,1,0:T(8,128)}, u32[]{:S(2)}) copy-start(s32[1,96,256]{2,1,0:T(8,128)} %param.8) | copy-start | bytes 294916
  0.0 16.4 %copy-start.2 = (s32[1,96,256]{2,1,0:T(8,128)S(1)}, s32[1,96,256]{2,1,0:T(8,128)}, u32[]{:S(2)}) copy-start(s32[1,96,256]{2,1,0:T(8,128)} %param.10) | copy-start | bytes 294916
  0.0 16.4 %copy-start.3 = (f32[1,96,256]{2,1,0:T(8,128)S(1)}, f32[1,96,256]{2,1,0:T(8,128)}, u32[]{:S(2)}) copy-start(f32[1,96,256]{2,1,0:T(8,128)} %param.11) | copy-start | bytes 294916
  0.0 16.4 %copy-start.5 = (f32[4096]{0:T(1024)S(1)}, f32[4096]{0:T(1024)}, u32[]{:S(2)}) copy-start(f32[4096]{0:T(1024)} %param.7) | copy-start | bytes 49156
  0.0 16.4 %copy-start.6 = (s32[1,96]{1,0:T(1,128)S(1)}, s32[1,96]{1,0:T(1,128)}, u32[]{:S(2)}) copy-start(s32[1,96]{1,0:T(1,128)} %count_ref.5) | copy-start | bytes 1156
  4.0 15.6 %collective-permute-start = (bf16[48,56,128]{2,1,0:T(8,128)(2,1)S(1)}, bf16[48,56,128]{2,1,0:T(8,128)(2,1)S(1)}, u32[]{:S(2)}, u32[]{:S(2)}) collective-permute-start(bf16[48,56,128]{2,1,0:T(8,128)(2,1)S(1)} %first_moments.1), channel_id=1, source_target_pairs={{0,8},{8,0},{1,9},{9,1},{2,10},{10,2},{3,11},{11,3},{4,12},{12,4},... | collective-permute-start | bytes 2064392 | tf_op jit(solution)/shard_map/ppermute | solution.py:304
  33.6 17.6 %copy-start.4 = (f32[7,128,128]{2,1,0:T(8,128)S(1)}, f32[7,128,128]{2,1,0:T(8,128)}, u32[]{:S(2)}) copy-start(f32[7,128,128]{2,1,0:T(8,128)} %green_ref.1) | copy-start | bytes 1376260
  76.6 9.9 %collective-permute-start.1 = (bf16[48,56,128]{2,1,0:T(8,128)(2,1)S(1)}, bf16[48,56,128]{2,1,0:T(8,128)(2,1)S(1)}, u32[]{:S(2)}, u32[]{:S(2)}) collective-permute-start(bf16[48,56,128]{2,1,0:T(8,128)(2,1)S(1)} %bitcast.17), channel_id=1, source_target_pairs={{0,8},{8,0},{1,9},{9,1},{2,10},{10,2},{3,11},{11,3},{4,12},{12,4},... | collective-permute-start | bytes 2064392 | tf_op jit(solution)/shard_map/ppermute | solution.py:304

commit v4 on v3

--- a/solution.py
+++ b/solution.py
@@ -13,7 +13,7 @@
 SLOTS = 256
 LANES = 128
 PTS = 4096
-HALF = 48
+HALF = X * Z
 BLOCK = 24
 STEPS = HALF // BLOCK
 HIGH, LOW = 32, 128
@@ -229,7 +229,7 @@
             precision=lax.Precision.HIGHEST,
             preferred_element_type=f32,
         )
-    table_ref[...] = jnp.broadcast_to(table.astype(bf16), (Z, ROWS, R))
+    table_ref[...] = jnp.broadcast_to(table.astype(bf16), (HALF, ROWS, R))
 
 
 VMEM = pl.BlockSpec(memory_space=pltpu.VMEM)
@@ -288,7 +288,7 @@
 def solved(parts, green):
     return pl.pallas_call(
         solve_kernel,
-        out_shape=pltpu.VMEM((Z, ROWS, R), bf16),
+        out_shape=pltpu.VMEM((HALF, ROWS, R), bf16),
         in_specs=[VMEM, VMEM],
         out_specs=VMEM,
         compiler_params=GRANT,
@@ -325,12 +325,8 @@
     tasks = [near(array) for array in tasks]
     kept = moments_of(own, count, near(rho), *tasks)
     chip = (kept + arrived.astype(f32)).astype(bf16)
-    along_x = exchanged(chip.reshape(X, Z, ROWS, R), "x").astype(f32)
-    plane = ((along_x[0] + along_x[1]) + (along_x[2] + along_x[3])).astype(bf16)
-    column = solved(near(exchanged(plane, "z")), near(green))
-
-    column = exchanged(column, "z")
-    half = exchanged(jnp.broadcast_to(column, (X, Z, ROWS, R)), "x").reshape(HALF, ROWS, R)
+    parts = exchanged(chip, ("x", "z"))
+    half = exchanged(solved(near(parts), near(green)), ("x", "z"))
     other_half = to_other_core(half)
     terms = evaluated(own, count, near(half), *tasks)
     terms = evaluated(other, count, near(other_half), *tasks, terms)

time: 103 us -> 119 us (1.16); the launches traced: 103 us -> 117 us
  blocking collectives: 69.2 us -> 85.2 us
  starting transfers between devices: 19.6 us -> 18.1 us
    all_to_all x5 -> x3, blocking collectives: 69.2 us -> 85.2 us  [exchanged(): return lax.all_to_all(array, axis, split_axis=0, concat_axis=0, tiled=True)]
    ppermute x2, starting transfers between devices: 19.6 us -> 18.1 us  [to_other_core(): return lax.ppermute(array, 'core', [(0, 1), (1, 0)])]
  transfers between devices with their start and end apart: 2 -> 2, of which waited for: 0 -> 0; matrix products, arithmetic and copies ran while one was open for 0% -> 0% of each run, Pallas kernels for 6% -> 5%
where the time goes in v4:
time: 119 us; the launch traced here: 117 us
  blocking collectives  85.2 us (72%)
  starting transfers between devices  18.1 us (15%)
  Pallas kernels  13 us (11%)
    all_to_all x3, blocking collectives, exchanged(): return lax.all_to_all(array, axis, split_axis=0, concat_axis=0, tiled=True)  85.2 us
    ppermute x2, starting transfers between devices, to_other_core(): return lax.ppermute(array, 'core', [(0, 1), (1, 0)])  18.1 us
    pallas_call x2, Pallas kernels, evaluated(): pl.pallas_call(evaluate_kernel, out_shape=pltpu.VMEM((HIGH, LOW), f32), i...  5.34 us
    pallas_call x1, Pallas kernels, first_moments_of(): pl.pallas_call(first_moments_kernel, out_shape=pltpu.VMEM((HALF, ROWS, R)...  3.95 us
    pallas_call x1, Pallas kernels, moments_of(): pl.pallas_call(moments_kernel, out_shape=pltpu.VMEM((HALF, ROWS, R), f32)...  3.13 us
  transfers between devices with their start and end apart: 2, of which 0 were waited for; matrix products, arithmetic and copies ran while one was open for 0% of the time, Pallas kernels for 5%

profile of v4, /device:TPU:1, one launch (start us, length us, event | category | flops | bytes accessed | tf_op | source)
XLA Modules:
  0.0 117.3 jit_solution(11374959592326212633)
XLA Ops:
  0.0 0.0 copy-start
  0.0 0.0 copy-start.1
  0.0 0.0 copy-start.2
  0.0 0.0 copy-start.3
  0.0 0.0 copy-start.5
  0.0 0.0 copy-start.6
  0.0 3.9 %first_moments.1 = bf16[48,56,128]{2,1,0:T(8,128)(2,1)S(1)} custom-call(s32[1]{0:T(128)S(6)} %sub.3.half_ref, s32[1,96]{1,0:T(1,128)} %count_ref.5, f32[32,128]{1,0:T(8,128)} %bitcast.25, s32[96,256]{1,0:T(8,128)} %bitcast.13, s32[96,256]{1,0:T(8,128)} %bitcast.17, f32[96,256]{1,0:T(8,128)} %bitcast.21, bf16[49,96,256]{2,1,0:T(8,128)(2,1)} %bitcast.9), custom_call_target="tpu_custom_call" | custom-call | tf_op jit(solution)/shard_map/first_moments/pallas_call | solution.py:242
  4.0 12.4 %collective-permute-start = (bf16[48,56,128]{2,1,0:T(8,128)(2,1)S(1)}, bf16[48,56,128]{2,1,0:T(8,128)(2,1)S(1)}, u32[]{:S(2)}, u32[]{:S(2)}) collective-permute-start(bf16[48,56,128]{2,1,0:T(8,128)(2,1)S(1)} %first_moments.1), channel_id=1, source_target_pairs={{0,8},{8,0},{1,9},{9,1},{2,10},{10,2},{3,11},{11,3},{4,12},{12,4},... | collective-permute-start | bytes 2064392 | tf_op jit(solution)/shard_map/ppermute | solution.py:304
  16.4 0.0 copy-done
  16.4 0.0 copy-done.1
  16.4 0.0 copy-done.2
  16.4 0.0 copy-done.3
  16.4 0.0 copy-done.5
  16.4 0.0 copy-done.6
  16.5 3.1 %moments.1 = f32[48,56,128]{2,1,0:T(8,128)S(1)} custom-call(s32[1]{0:T(128)} %bitcast.half_ref, s32[1,96]{1,0:T(1,128)S(1)} %copy-done.6, f32[32,128]{1,0:T(8,128)S(1)} %bitcast.26, s32[96,256]{1,0:T(8,128)S(1)} %bitcast.14, s32[96,256]{1,0:T(8,128)S(1)} %bitcast.18, f32[96,256]{1,0:T(8,128)S(1)} %bitcast.22, bf16[49,96,256]{2,1,0:T(8,128)(2,1)S(1)} %bitcast.10), custom_call_target="tpu_custom_call" | custom-call | tf_op jit(solution)/shard_map/moments/pallas_call | solution.py:265
  19.6 0.0 collective-permute-done
  19.6 0.2 add_convert_fusion
  19.8 0.0 copy-start.4
  19.8 37.4 %all_to_all.19.parts_ref = bf16[48,56,128]{2,1,0:T(8,128)(2,1)S(1)} all-to-all(bf16[48,56,128]{2,1,0:T(8,128)(2,1)S(1)} %add_convert_fusion), channel_id=1, replica_groups=mesh['x'=4,'z'=12,'core'=2,'atom'=8] {'x','z'}, dimensions={0} | all-to-all | bytes 1376256 | tf_op jit(solution)/shard_map/all_to_all | solution.py:300
  57.2 0.0 copy-done.4
  57.2 0.6 solve.1
  57.8 34.5 %all_to_all.20.table_ref = bf16[48,56,128]{2,1,0:T(8,128)(2,1)S(1)} all-to-all(bf16[48,56,128]{2,1,0:T(8,128)(2,1)S(1)} %solve.1), channel_id=1, replica_groups=mesh['x'=4,'z'=12,'core'=2,'atom'=8] {'x','z'}, dimensions={0} | all-to-all | bytes 1376256 | tf_op jit(solution)/shard_map/all_to_all | solution.py:300
  92.4 5.7 %collective-permute-start.1 = (bf16[48,56,128]{2,1,0:T(8,128)(2,1)S(1)}, bf16[48,56,128]{2,1,0:T(8,128)(2,1)S(1)}, u32[]{:S(2)}, u32[]{:S(2)}) collective-permute-start(bf16[48,56,128]{2,1,0:T(8,128)(2,1)S(1)} %all_to_all.20.table_ref), channel_id=1, source_target_pairs={{0,8},{8,0},{1,9},{9,1},{2,10},{10,2},{3,11},{11,3},{4,12},{12,4},... | collective-permute-start | bytes 2064392 | tf_op jit(solution)/shard_map/ppermute | solution.py:304
  98.1 2.7 %evaluate.2.refs_0_ = f32[32,128]{1,0:T(8,128)S(1)} custom-call(s32[1]{0:T(128)} %bitcast.half_ref, s32[1,96]{1,0:T(1,128)S(1)} %copy-done.6, bf16[48,56,128]{2,1,0:T(8,128)(2,1)S(1)} %all_to_all.20.table_ref, s32[96,256]{1,0:T(8,128)S(1)} %bitcast.15, s32[96,256]{1,0:T(8,128)S(1)} %bitcast.19, f32[96,256]{1,0:T(8,128)S(1)} %bitcast.23, ...), custom_call_target="tpu_custom_call" | custom-call | tf_op jit(solution)/shard_map/evaluate/pallas_call | solution.py:277
  100.8 0.0 collective-permute-done.1.table_ref
  100.8 2.7 %evaluate.3 = f32[32,128]{1,0:T(8,128)S(1)} custom-call(s32[1]{0:T(128)S(6)} %sub.3.half_ref, s32[1,96]{1,0:T(1,128)S(1)} %copy-done.6, bf16[48,56,128]{2,1,0:T(8,128)(2,1)S(1)} %collective-permute-done.1.table_ref, s32[96,256]{1,0:T(8,128)S(1)} %bitcast.16, s32[96,256]{1,0:T(8,128)S(1)} %bitcast.20, f32[96,256]{1,0:T(8,128)S(1)} %bitcast.24, ...), custom_call_target="tpu_custom_call" | custom-call | tf_op jit(solution)/shard_map/evaluate/pallas_call | solution.py:277
  103.5 13.2 %all_to_all.21 = f32[8,1,512]{2,1,0:T(1,128)S(1)} all-to-all(f32[8,1,512]{2,1,0:T(1,128)S(1)} %bitcast.27), channel_id=1, replica_groups=mesh['x'=4,'z'=12,'core'=2,'atom'=8] {'atom'}, dimensions={0} | all-to-all | bytes 32768 | tf_op jit(solution)/shard_map/all_to_all | solution.py:300
  116.7 0.6 reduce_sum.9
Async XLA Ops:
  0.0 16.4 %copy-start = (bf16[1,96,49,256]{3,1,2,0:T(8,128)(2,1)S(1)}, bf16[1,96,49,256]{3,1,2,0:T(8,128)(2,1)}, u32[]{:S(2)}) copy-start(bf16[1,96,49,256]{3,1,2,0:T(8,128)(2,1)} %param.12) | copy-start | bytes 7225348
  0.0 16.4 %copy-start.1 = (s32[1,96,256]{2,1,0:T(8,128)S(1)}, s32[1,96,256]{2,1,0:T(8,128)}, u32[]{:S(2)}) copy-start(s32[1,96,256]{2,1,0:T(8,128)} %param.8) | copy-start | bytes 294916
  0.0 16.4 %copy-start.2 = (s32[1,96,256]{2,1,0:T(8,128)S(1)}, s32[1,96,256]{2,1,0:T(8,128)}, u32[]{:S(2)}) copy-start(s32[1,96,256]{2,1,0:T(8,128)} %param.10) | copy-start | bytes 294916
  0.0 16.4 %copy-start.3 = (f32[1,96,256]{2,1,0:T(8,128)S(1)}, f32[1,96,256]{2,1,0:T(8,128)}, u32[]{:S(2)}) copy-start(f32[1,96,256]{2,1,0:T(8,128)} %param.11) | copy-start | bytes 294916
  0.0 16.4 %copy-start.5 = (f32[4096]{0:T(1024)S(1)}, f32[4096]{0:T(1024)}, u32[]{:S(2)}) copy-start(f32[4096]{0:T(1024)} %param.7) | copy-start | bytes 49156
  0.0 16.4 %copy-start.6 = (s32[1,96]{1,0:T(1,128)S(1)}, s32[1,96]{1,0:T(1,128)}, u32[]{:S(2)}) copy-start(s32[1,96]{1,0:T(1,128)} %count_ref.5) | copy-start | bytes 1156
  4.0 15.6 %collective-permute-start = (bf16[48,56,128]{2,1,0:T(8,128)(2,1)S(1)}, bf16[48,56,128]{2,1,0:T(8,128)(2,1)S(1)}, u32[]{:S(2)}, u32[]{:S(2)}) collective-permute-start(bf16[48,56,128]{2,1,0:T(8,128)(2,1)S(1)} %first_moments.1), channel_id=1, source_target_pairs={{0,8},{8,0},{1,9},{9,1},{2,10},{10,2},{3,11},{11,3},{4,12},{12,4},... | collective-permute-start | bytes 2064392 | tf_op jit(solution)/shard_map/ppermute | solution.py:304
  19.8 37.5 %copy-start.4 = (f32[7,128,128]{2,1,0:T(8,128)S(1)}, f32[7,128,128]{2,1,0:T(8,128)}, u32[]{:S(2)}) copy-start(f32[7,128,128]{2,1,0:T(8,128)} %green_ref.1) | copy-start | bytes 1376260
  92.4 8.4 %collective-permute-start.1 = (bf16[48,56,128]{2,1,0:T(8,128)(2,1)S(1)}, bf16[48,56,128]{2,1,0:T(8,128)(2,1)S(1)}, u32[]{:S(2)}, u32[]{:S(2)}) collective-permute-start(bf16[48,56,128]{2,1,0:T(8,128)(2,1)S(1)} %all_to_all.20.table_ref), channel_id=1, source_target_pairs={{0,8},{8,0},{1,9},{9,1},{2,10},{10,2},{3,11},{11,3},{4,12},{12,4},... | collective-permute-start | bytes 2064392 | tf_op jit(solution)/shard_map/ppermute | solution.py:304

commit v5 on v4

--- a/solution.py
+++ b/solution.py
@@ -5,7 +5,8 @@
 from jax.experimental.pallas import tpu as pltpu
 from jax.sharding import Mesh, PartitionSpec as P
 
-X, Z, CORES = 4, 12, 2
+X, BLOCKS, PARTS, CORES = 4, 4, 3, 2
+IN_BLOCK = X * PARTS
 LMAX = 6
 LM = 49
 ROWS = 56
@@ -13,7 +14,7 @@
 SLOTS = 256
 LANES = 128
 PTS = 4096
-HALF = X * Z
+HALF = IN_BLOCK * BLOCKS
 BLOCK = 24
 STEPS = HALF // BLOCK
 HIGH, LOW = 32, 128
@@ -217,19 +218,31 @@
     out_ref[...] = total + before_ref[0][...] if before_ref else total
 
 
+def sum_kernel(arrived_ref, out_ref):
+    for n in range(BLOCKS):
+        plane = jnp.sum(arrived_ref[:, n].astype(f32), axis=0).astype(bf16)
+        out_ref[:, n] = jnp.broadcast_to(plane, (BLOCKS, ROWS, R))
+
+
 def solve_kernel(parts_ref, green_ref, table_ref):
     moments = jnp.sum(parts_ref[...].astype(f32), axis=0)
-    row = lax.broadcasted_iota(jnp.int32, (ROWS, R), 0)
-    table = jnp.zeros((ROWS, R), f32)
+    tiles = [jnp.zeros((BLOCKS, 8, R), f32)] * (ROWS // 8)
     for degree in range(LMAX + 1):
-        of_degree = (row >= degree * degree) & (row < (degree + 1) * (degree + 1))
-        table = table + jnp.dot(
-            jnp.where(of_degree, moments, 0.0),
+        start, stop = degree * degree, (degree + 1) * (degree + 1)
+        first, last = start // 8, (stop - 1) // 8 + 1
+        count = (last - first) * 8
+        row = lax.broadcasted_iota(jnp.int32, (BLOCKS, count, R), 1) + first * 8
+        of_degree = jnp.where((row >= start) & (row < stop), moments[:, first * 8 : last * 8], 0.0)
+        solved = jnp.dot(
+            of_degree.reshape(BLOCKS * count, R),
             green_ref[degree],
             precision=lax.Precision.HIGHEST,
             preferred_element_type=f32,
-        )
-    table_ref[...] = jnp.broadcast_to(table.astype(bf16), (HALF, ROWS, R))
+        ).reshape(BLOCKS, count, R)
+        for tile in range(first, last):
+            tiles[tile] = tiles[tile] + solved[:, (tile - first) * 8 : (tile - first + 1) * 8]
+    table = jnp.concatenate(tiles, axis=1).astype(bf16)
+    table_ref[...] = jnp.broadcast_to(table, (IN_BLOCK, BLOCKS, ROWS, R))
 
 
 VMEM = pl.BlockSpec(memory_space=pltpu.VMEM)
@@ -285,10 +298,21 @@
     )(half, count, table, points, index, fraction, angular, *before)
 
 
+def summed(arrived):
+    return pl.pallas_call(
+        sum_kernel,
+        out_shape=pltpu.VMEM((BLOCKS, BLOCKS, ROWS, R), bf16),
+        in_specs=[VMEM],
+        out_specs=VMEM,
+        compiler_params=GRANT,
+        name="sum",
+    )(arrived)
+
+
 def solved(parts, green):
     return pl.pallas_call(
         solve_kernel,
-        out_shape=pltpu.VMEM((HALF, ROWS, R), bf16),
+        out_shape=pltpu.VMEM((IN_BLOCK, BLOCKS, ROWS, R), bf16),
         in_specs=[VMEM, VMEM],
         out_specs=VMEM,
         compiler_params=GRANT,
@@ -325,8 +349,9 @@
     tasks = [near(array) for array in tasks]
     kept = moments_of(own, count, near(rho), *tasks)
     chip = (kept + arrived.astype(f32)).astype(bf16)
-    parts = exchanged(chip, ("x", "z"))
-    half = exchanged(solved(near(parts), near(green)), ("x", "z"))
+    arrived = exchanged(chip.reshape(IN_BLOCK, BLOCKS, ROWS, R), ("x", "part"))
+    parts = exchanged(summed(near(arrived)), "block")
+    half = exchanged(solved(near(parts), near(green)), ("x", "part")).reshape(HALF, ROWS, R)
     other_half = to_other_core(half)
     terms = evaluated(own, count, near(half), *tasks)
     terms = evaluated(other, count, near(other_half), *tasks, terms)
@@ -334,8 +359,8 @@
 
 
 def solution(mesh):
-    mesh = Mesh(mesh.devices.reshape(X, Z, CORES, 8), ("x", "z", "core", "atom"))
-    shell = ("x", "z", "core")
+    mesh = Mesh(mesh.devices.reshape(X, BLOCKS, PARTS, CORES, 8), ("x", "block", "part", "core", "atom"))
+    shell = ("x", "block", "part", "core")
     in_specs = (
         P(shell),
         P(shell, "atom", None),

time: 119 us -> 99.2 us (0.83); the launches traced: 117 us -> 98.9 us
  blocking collectives: 85.2 us -> 64.6 us
  starting transfers between devices: 18.1 us -> 20.3 us
    all_to_all x3 -> x4, blocking collectives: 85.2 us -> 64.6 us  [exchanged(): return lax.all_to_all(array, axis, split_axis=0, concat_axis=0, tiled=True)]
    ppermute x2, starting transfers between devices: 18.1 us -> 20.3 us  [to_other_core(): return lax.ppermute(array, 'core', [(0, 1), (1, 0)])]
  transfers between devices with their start and end apart: 2 -> 2, of which waited for: 0 -> 0; matrix products, arithmetic and copies ran while one was open for 0% -> 0% of each run, Pallas kernels for 5% -> 6%
where the time goes in v5:
time: 99.2 us; the launch traced here: 98.9 us
  blocking collectives  64.6 us (65%)
  starting transfers between devices  20.3 us (20%)
  Pallas kernels  13 us (13%)
    all_to_all x4, blocking collectives, exchanged(): return lax.all_to_all(array, axis, split_axis=0, concat_axis=0, tiled=True)  64.6 us
    ppermute x2, starting transfers between devices, to_other_core(): return lax.ppermute(array, 'core', [(0, 1), (1, 0)])  20.3 us
    pallas_call x2, Pallas kernels, evaluated(): pl.pallas_call(evaluate_kernel, out_shape=pltpu.VMEM((HIGH, LOW), f32), i...  5.34 us
    pallas_call x1, Pallas kernels, first_moments_of(): pl.pallas_call(first_moments_kernel, out_shape=pltpu.VMEM((HALF, ROWS, R)...  3.95 us
    pallas_call x1, Pallas kernels, moments_of(): pl.pallas_call(moments_kernel, out_shape=pltpu.VMEM((HALF, ROWS, R), f32)...  3.13 us
  transfers between devices with their start and end apart: 2, of which 0 were waited for; matrix products, arithmetic and copies ran while one was open for 0% of the time, Pallas kernels for 6%

profile of v5, /device:TPU:1, one launch (start us, length us, event | category | flops | bytes accessed | tf_op | source)
XLA Modules:
  0.0 98.9 jit_solution(11104092207844961270)
XLA Ops:
  0.0 0.0 copy-start
  0.0 0.0 copy-start.1
  0.0 0.0 copy-start.2
  0.0 0.0 copy-start.3
  0.0 0.0 copy-start.5
  0.0 0.0 copy-start.6
  0.0 3.9 %first_moments.1 = bf16[48,56,128]{2,1,0:T(8,128)(2,1)S(1)} custom-call(s32[1]{0:T(128)S(6)} %sub.3.half_ref, s32[1,96]{1,0:T(1,128)} %count_ref.5, f32[32,128]{1,0:T(8,128)} %bitcast.29, s32[96,256]{1,0:T(8,128)} %bitcast.17, s32[96,256]{1,0:T(8,128)} %bitcast.21, f32[96,256]{1,0:T(8,128)} %bitcast.25, bf16[49,96,256]{2,1,0:T(8,128)(2,1)} %bitcast.11), custom_call_target="tpu_custom_call" | custom-call | tf_op jit(solution)/shard_map/first_moments/pallas_call | solution.py:255
  4.0 12.4 %collective-permute-start = (bf16[48,56,128]{2,1,0:T(8,128)(2,1)S(1)}, bf16[48,56,128]{2,1,0:T(8,128)(2,1)S(1)}, u32[]{:S(2)}, u32[]{:S(2)}) collective-permute-start(bf16[48,56,128]{2,1,0:T(8,128)(2,1)S(1)} %first_moments.1), channel_id=1, source_target_pairs={{0,8},{8,0},{1,9},{9,1},{2,10},{10,2},{3,11},{11,3},{4,12},{12,4},... | collective-permute-start | bytes 2064392 | tf_op jit(solution)/shard_map/ppermute | solution.py:328
  16.4 0.0 copy-done
  16.4 0.0 copy-done.1
  16.4 0.0 copy-done.2
  16.4 0.0 copy-done.3
  16.4 0.0 copy-done.5
  16.4 0.0 copy-done.6
  16.5 3.1 %moments.1 = f32[48,56,128]{2,1,0:T(8,128)S(1)} custom-call(s32[1]{0:T(128)} %bitcast.half_ref, s32[1,96]{1,0:T(1,128)S(1)} %copy-done.6, f32[32,128]{1,0:T(8,128)S(1)} %bitcast.30, s32[96,256]{1,0:T(8,128)S(1)} %bitcast.18, s32[96,256]{1,0:T(8,128)S(1)} %bitcast.22, f32[96,256]{1,0:T(8,128)S(1)} %bitcast.26, bf16[49,96,256]{2,1,0:T(8,128)(2,1)S(1)} %bitcast.12), custom_call_target="tpu_custom_call" | custom-call | tf_op jit(solution)/shard_map/moments/pallas_call | solution.py:278
  19.6 0.0 collective-permute-done
  19.6 0.2 add_convert_fusion
  19.8 0.0 copy-start.4
  19.8 17.4 %all_to_all.24.arrived_ref = bf16[12,4,56,128]{3,2,1,0:T(8,128)(2,1)S(1)} all-to-all(bf16[12,4,56,128]{3,2,1,0:T(8,128)(2,1)S(1)} %bitcast.32), channel_id=1, replica_groups=mesh['x'=4,'block'=4,'part'=3,'core'=2,'atom'=8] {'x','part'}, dimensions={0} | all-to-all | bytes 1376256 | tf_op jit(solution)/shard_map/all_to_all | solution.py:324
  37.2 0.1 sum.1
  37.3 20.9 %all_to_all.25.parts_ref = bf16[4,4,56,128]{3,2,1,0:T(8,128)(2,1)S(1)} all-to-all(bf16[4,4,56,128]{3,2,1,0:T(8,128)(2,1)S(1)} %sum.1), channel_id=1, replica_groups=mesh['x'=4,'block'=4,'part'=3,'core'=2,'atom'=8] {'block'}, dimensions={0} | all-to-all | bytes 458752 | tf_op jit(solution)/shard_map/all_to_all | solution.py:324
  58.2 0.0 copy-done.4
  58.2 0.5 solve.1
  58.7 13.1 %all_to_all.26 = bf16[12,4,56,128]{3,2,1,0:T(8,128)(2,1)S(1)} all-to-all(bf16[12,4,56,128]{3,2,1,0:T(8,128)(2,1)S(1)} %solve.1), channel_id=1, replica_groups=mesh['x'=4,'block'=4,'part'=3,'core'=2,'atom'=8] {'x','part'}, dimensions={0} | all-to-all | bytes 1376256 | tf_op jit(solution)/shard_map/all_to_all | solution.py:324
  71.8 7.9 %collective-permute-start.1 = (bf16[48,56,128]{2,1,0:T(8,128)(2,1)S(1)}, bf16[48,56,128]{2,1,0:T(8,128)(2,1)S(1)}, u32[]{:S(2)}, u32[]{:S(2)}) collective-permute-start(bf16[48,56,128]{2,1,0:T(8,128)(2,1)S(1)} %bitcast.15), channel_id=1, source_target_pairs={{0,8},{8,0},{1,9},{9,1},{2,10},{10,2},{3,11},{11,3},{4,12},{12,4},... | collective-permute-start | bytes 2064392 | tf_op jit(solution)/shard_map/ppermute | solution.py:328
  79.7 2.7 %evaluate.2.refs_0_ = f32[32,128]{1,0:T(8,128)S(1)} custom-call(s32[1]{0:T(128)} %bitcast.half_ref, s32[1,96]{1,0:T(1,128)S(1)} %copy-done.6, bf16[48,56,128]{2,1,0:T(8,128)(2,1)S(1)} %bitcast.16, s32[96,256]{1,0:T(8,128)S(1)} %bitcast.19, s32[96,256]{1,0:T(8,128)S(1)} %bitcast.23, f32[96,256]{1,0:T(8,128)S(1)} %bitcast.27, bf16[49,96,256]{2,1,0:T(8,128)(2,1)S(1)} %bitcast.13), custom_call_target="tpu_custom_call" | custom-call | tf_op jit(solution)/shard_map/evaluate/pallas_call | solution.py:290
  82.4 0.0 collective-permute-done.1.table_ref
  82.4 2.7 %evaluate.3 = f32[32,128]{1,0:T(8,128)S(1)} custom-call(s32[1]{0:T(128)S(6)} %sub.3.half_ref, s32[1,96]{1,0:T(1,128)S(1)} %copy-done.6, bf16[48,56,128]{2,1,0:T(8,128)(2,1)S(1)} %collective-permute-done.1.table_ref, s32[96,256]{1,0:T(8,128)S(1)} %bitcast.20, s32[96,256]{1,0:T(8,128)S(1)} %bitcast.24, f32[96,256]{1,0:T(8,128)S(1)} %bitcast.28, ...), custom_call_target="tpu_custom_call" | custom-call | tf_op jit(solution)/shard_map/evaluate/pallas_call | solution.py:290
  85.1 13.2 %all_to_all.27 = f32[8,1,512]{2,1,0:T(1,128)S(1)} all-to-all(f32[8,1,512]{2,1,0:T(1,128)S(1)} %bitcast.31), channel_id=1, replica_groups=mesh['x'=4,'block'=4,'part'=3,'core'=2,'atom'=8] {'atom'}, dimensions={0} | all-to-all | bytes 32768 | tf_op jit(solution)/shard_map/all_to_all | solution.py:324
  98.3 0.6 reduce_sum.9
Async XLA Ops:
  0.0 16.4 %copy-start = (bf16[1,96,49,256]{3,1,2,0:T(8,128)(2,1)S(1)}, bf16[1,96,49,256]{3,1,2,0:T(8,128)(2,1)}, u32[]{:S(2)}) copy-start(bf16[1,96,49,256]{3,1,2,0:T(8,128)(2,1)} %param.12) | copy-start | bytes 7225348
  0.0 16.4 %copy-start.1 = (s32[1,96,256]{2,1,0:T(8,128)S(1)}, s32[1,96,256]{2,1,0:T(8,128)}, u32[]{:S(2)}) copy-start(s32[1,96,256]{2,1,0:T(8,128)} %param.8) | copy-start | bytes 294916
  0.0 16.4 %copy-start.2 = (s32[1,96,256]{2,1,0:T(8,128)S(1)}, s32[1,96,256]{2,1,0:T(8,128)}, u32[]{:S(2)}) copy-start(s32[1,96,256]{2,1,0:T(8,128)} %param.10) | copy-start | bytes 294916
  0.0 16.4 %copy-start.3 = (f32[1,96,256]{2,1,0:T(8,128)S(1)}, f32[1,96,256]{2,1,0:T(8,128)}, u32[]{:S(2)}) copy-start(f32[1,96,256]{2,1,0:T(8,128)} %param.11) | copy-start | bytes 294916
  0.0 16.4 %copy-start.5 = (f32[4096]{0:T(1024)S(1)}, f32[4096]{0:T(1024)}, u32[]{:S(2)}) copy-start(f32[4096]{0:T(1024)} %param.7) | copy-start | bytes 49156
  0.0 16.4 %copy-start.6 = (s32[1,96]{1,0:T(1,128)S(1)}, s32[1,96]{1,0:T(1,128)}, u32[]{:S(2)}) copy-start(s32[1,96]{1,0:T(1,128)} %count_ref.5) | copy-start | bytes 1156
  4.0 15.6 %collective-permute-start = (bf16[48,56,128]{2,1,0:T(8,128)(2,1)S(1)}, bf16[48,56,128]{2,1,0:T(8,128)(2,1)S(1)}, u32[]{:S(2)}, u32[]{:S(2)}) collective-permute-start(bf16[48,56,128]{2,1,0:T(8,128)(2,1)S(1)} %first_moments.1), channel_id=1, source_target_pairs={{0,8},{8,0},{1,9},{9,1},{2,10},{10,2},{3,11},{11,3},{4,12},{12,4},... | collective-permute-start | bytes 2064392 | tf_op jit(solution)/shard_map/ppermute | solution.py:328
  19.8 38.4 %copy-start.4 = (f32[7,128,128]{2,1,0:T(8,128)S(1)}, f32[7,128,128]{2,1,0:T(8,128)}, u32[]{:S(2)}) copy-start(f32[7,128,128]{2,1,0:T(8,128)} %green_ref.1) | copy-start | bytes 1376260
  71.8 10.6 %collective-permute-start.1 = (bf16[48,56,128]{2,1,0:T(8,128)(2,1)S(1)}, bf16[48,56,128]{2,1,0:T(8,128)(2,1)S(1)}, u32[]{:S(2)}, u32[]{:S(2)}) collective-permute-start(bf16[48,56,128]{2,1,0:T(8,128)(2,1)S(1)} %bitcast.15), channel_id=1, source_target_pairs={{0,8},{8,0},{1,9},{9,1},{2,10},{10,2},{3,11},{11,3},{4,12},{12,4},... | collective-permute-start | bytes 2064392 | tf_op jit(solution)/shard_map/ppermute | solution.py:328

commit v6 on v5

--- a/solution.py
+++ b/solution.py
@@ -241,8 +241,15 @@
         ).reshape(BLOCKS, count, R)
         for tile in range(first, last):
             tiles[tile] = tiles[tile] + solved[:, (tile - first) * 8 : (tile - first + 1) * 8]
-    table = jnp.concatenate(tiles, axis=1).astype(bf16)
-    table_ref[...] = jnp.broadcast_to(table, (IN_BLOCK, BLOCKS, ROWS, R))
+    table_ref[...] = jnp.concatenate(tiles, axis=1).astype(bf16)
+
+
+def join_kernel(part_ref, own_ref, below_ref, above_ref, out_ref):
+    part = part_ref[0]
+    places = (part, jnp.where(part == 0, PARTS - 1, part - 1), jnp.where(part == PARTS - 1, 0, part + 1))
+    for place, tables_ref in zip(places, (own_ref, below_ref, above_ref)):
+        for n in range(X):
+            out_ref[n, place] = tables_ref[...]
 
 
 VMEM = pl.BlockSpec(memory_space=pltpu.VMEM)
@@ -312,12 +319,28 @@
 def solved(parts, green):
     return pl.pallas_call(
         solve_kernel,
-        out_shape=pltpu.VMEM((IN_BLOCK, BLOCKS, ROWS, R), bf16),
+        out_shape=pltpu.VMEM((BLOCKS, ROWS, R), bf16),
         in_specs=[VMEM, VMEM],
         out_specs=VMEM,
         compiler_params=GRANT,
         name="solve",
     )(parts, green)
+
+
+def joined(part, own, below, above):
+    return pl.pallas_call(
+        join_kernel,
+        out_shape=pltpu.VMEM((X, PARTS, BLOCKS, ROWS, R), bf16),
+        in_specs=[SMEM] + [VMEM] * 3,
+        out_specs=VMEM,
+        compiler_params=GRANT,
+        name="join",
+    )(part, own, below, above)
+
+
+def along_z(array, step):
+    count = BLOCKS * PARTS
+    return lax.ppermute(array, ("block", "part"), [(z, (z + step) % count) for z in range(count)])
 
 
 def exchanged(array, axis):
@@ -351,7 +374,10 @@
     chip = (kept + arrived.astype(f32)).astype(bf16)
     arrived = exchanged(chip.reshape(IN_BLOCK, BLOCKS, ROWS, R), ("x", "part"))
     parts = exchanged(summed(near(arrived)), "block")
-    half = exchanged(solved(near(parts), near(green)), ("x", "part")).reshape(HALF, ROWS, R)
+    tables = solved(near(parts), near(green))
+    part = lax.axis_index("part").astype(jnp.int32).reshape(1)
+    column = joined(part, tables, along_z(tables, 1), along_z(tables, -1))
+    half = exchanged(column, "x").reshape(HALF, ROWS, R)
     other_half = to_other_core(half)
     terms = evaluated(own, count, near(half), *tasks)
     terms = evaluated(other, count, near(other_half), *tasks, terms)

time: 99.2 us -> 105 us (1.058)
  waiting for transfers between devices: 0.01 us -> 4.18 us
  starting transfers between devices: 20.3 us -> 24.3 us
  blocking collectives: 64.6 us -> 61.7 us
    ppermute x0 -> x2, starting transfers between devices: none -> 5.28 us  [along_z(): lax.ppermute(array, ('block', 'part'), [(z, (z + step) % count) for z in...]
    ppermute x0 -> x2, waiting for transfers between devices: none -> 4.17 us  [along_z(): lax.ppermute(array, ('block', 'part'), [(z, (z + step) % count) for z in...]
    all_to_all x4, blocking collectives: 64.6 us -> 61.7 us  [exchanged(): return lax.all_to_all(array, axis, split_axis=0, concat_axis=0, tiled=True)]
    ppermute x2, starting transfers between devices: 20.3 us -> 19 us  [to_other_core(): return lax.ppermute(array, 'core', [(0, 1), (1, 0)])]
  transfers between devices with their start and end apart: 2 -> 4, of which waited for: 0 -> 1; matrix products, arithmetic and copies ran while one was open for 0% -> 0% of each run, Pallas kernels for 6% -> 6%
where the time goes in v6:
time: 105 us; the launch traced here: 104 us
  blocking collectives  61.7 us (59%)
  starting transfers between devices  24.3 us (23%)
  Pallas kernels  13.1 us (12%)
  waiting for transfers between devices  4.18 us (4%)
    all_to_all x4, blocking collectives, exchanged(): return lax.all_to_all(array, axis, split_axis=0, concat_axis=0, tiled=True)  61.7 us
    ppermute x2, starting transfers between devices, to_other_core(): return lax.ppermute(array, 'core', [(0, 1), (1, 0)])  19 us
    pallas_call x2, Pallas kernels, evaluated(): pl.pallas_call(evaluate_kernel, out_shape=pltpu.VMEM((HIGH, LOW), f32), i...  5.35 us
    ppermute x2, starting transfers between devices, along_z(): lax.ppermute(array, ('block', 'part'), [(z, (z + step) % count) for z in...  5.28 us
    ppermute x2, waiting for transfers between devices, along_z(): lax.ppermute(array, ('block', 'part'), [(z, (z + step) % count) for z in...  4.17 us
    pallas_call x1, Pallas kernels, first_moments_of(): pl.pallas_call(first_moments_kernel, out_shape=pltpu.VMEM((HALF, ROWS, R)...  3.95 us
    pallas_call x1, Pallas kernels, moments_of(): pl.pallas_call(moments_kernel, out_shape=pltpu.VMEM((HALF, ROWS, R), f32)...  3.14 us
  transfers between devices with their start and end apart: 4, of which 1 were waited for; matrix products, arithmetic and copies ran while one was open for 0% of the time, Pallas kernels for 6%

profile of v6, /device:TPU:1, one launch (start us, length us, event | category | flops | bytes accessed | tf_op | source)
XLA Modules:
  0.0 104.3 jit_solution(2164763078740861571)
XLA Ops:
  0.0 0.0 copy-start.3
  0.0 0.0 copy-start.5
  0.0 0.0 copy-start.6
  0.0 3.9 %first_moments.1 = bf16[48,56,128]{2,1,0:T(8,128)(2,1)S(1)} custom-call(s32[1]{0:T(128)S(6)} %sub.3.half_ref, s32[1,96]{1,0:T(1,128)} %count_ref.5, f32[32,128]{1,0:T(8,128)} %bitcast.30, s32[96,256]{1,0:T(8,128)} %bitcast.18, s32[96,256]{1,0:T(8,128)} %bitcast.22, f32[96,256]{1,0:T(8,128)} %bitcast.26, bf16[49,96,256]{2,1,0:T(8,128)(2,1)} %bitcast.12), custom_call_target="tpu_custom_call" | custom-call | tf_op jit(solution)/shard_map/first_moments/pallas_call | solution.py:262
  4.0 12.4 %collective-permute-start = (bf16[48,56,128]{2,1,0:T(8,128)(2,1)S(1)}, bf16[48,56,128]{2,1,0:T(8,128)(2,1)S(1)}, u32[]{:S(2)}, u32[]{:S(2)}) collective-permute-start(bf16[48,56,128]{2,1,0:T(8,128)(2,1)S(1)} %first_moments.1), channel_id=1, source_target_pairs={{0,8},{8,0},{1,9},{9,1},{2,10},{10,2},{3,11},{11,3},{4,12},{12,4},... | collective-permute-start | bytes 2064392 | tf_op jit(solution)/shard_map/ppermute | solution.py:351
  16.4 0.0 copy-done
  16.4 0.0 copy-done.1
  16.4 0.0 copy-done.2
  16.4 0.0 copy-done.3
  16.4 0.0 copy-done.5
  16.4 0.0 copy-done.6
  16.5 3.1 %moments.1 = f32[48,56,128]{2,1,0:T(8,128)S(1)} custom-call(s32[1]{0:T(128)} %bitcast.half_ref, s32[1,96]{1,0:T(1,128)S(1)} %copy-done.6, f32[32,128]{1,0:T(8,128)S(1)} %bitcast.31, s32[96,256]{1,0:T(8,128)S(1)} %bitcast.19, s32[96,256]{1,0:T(8,128)S(1)} %bitcast.23, f32[96,256]{1,0:T(8,128)S(1)} %bitcast.27, bf16[49,96,256]{2,1,0:T(8,128)(2,1)S(1)} %bitcast.13), custom_call_target="tpu_custom_call" | custom-call | tf_op jit(solution)/shard_map/moments/pallas_call | solution.py:285
  19.6 0.0 collective-permute-done
  19.6 0.1 add_convert_fusion
  19.8 0.0 copy-start.4
  19.8 17.4 %all_to_all.24.arrived_ref = bf16[12,4,56,128]{3,2,1,0:T(8,128)(2,1)S(1)} all-to-all(bf16[12,4,56,128]{3,2,1,0:T(8,128)(2,1)S(1)} %bitcast.33), channel_id=1, replica_groups=mesh['x'=4,'block'=4,'part'=3,'core'=2,'atom'=8] {'x','part'}, dimensions={0} | all-to-all | bytes 1376256 | tf_op jit(solution)/shard_map/all_to_all | solution.py:347
  37.2 0.1 sum.1
  37.3 20.9 %all_to_all.25.parts_ref = bf16[4,4,56,128]{3,2,1,0:T(8,128)(2,1)S(1)} all-to-all(bf16[4,4,56,128]{3,2,1,0:T(8,128)(2,1)S(1)} %sum.1), channel_id=1, replica_groups=mesh['x'=4,'block'=4,'part'=3,'core'=2,'atom'=8] {'block'}, dimensions={0} | all-to-all | bytes 458752 | tf_op jit(solution)/shard_map/all_to_all | solution.py:347
  58.2 0.0 copy-done.4
  58.2 0.5 solve.1.own_ref
  58.7 1.9 %collective-permute-start.2 = (bf16[4,56,128]{2,1,0:T(8,128)(2,1)S(1)}, bf16[4,56,128]{2,1,0:T(8,128)(2,1)S(1)}, u32[]{:S(2)}, u32[]{:S(2)}) collective-permute-start(bf16[4,56,128]{2,1,0:T(8,128)(2,1)S(1)} %solve.1.own_ref), channel_id=1, source_target_pairs={{0,176},{16,0},{32,16},{48,32},{64,48},{80,64},{96,80},{112,96},{1... | collective-permute-start | bytes 172040 | tf_op jit(solution)/shard_map/ppermute | solution.py:343
  60.6 3.4 %collective-permute-start.1 = (bf16[4,56,128]{2,1,0:T(8,128)(2,1)S(1)}, bf16[4,56,128]{2,1,0:T(8,128)(2,1)S(1)}, u32[]{:S(2)}, u32[]{:S(2)}) collective-permute-start(bf16[4,56,128]{2,1,0:T(8,128)(2,1)S(1)} %solve.1.own_ref), channel_id=1, source_target_pairs={{0,16},{16,32},{32,48},{48,64},{64,80},{80,96},{96,112},{112,128},... | collective-permute-start | bytes 172040 | tf_op jit(solution)/shard_map/ppermute | solution.py:343
  64.0 0.0 collective-permute-done.2.above_ref
  64.0 4.2 %collective-permute-done.1.below_ref = bf16[4,56,128]{2,1,0:T(8,128)(2,1)S(1)} collective-permute-done((bf16[4,56,128]{2,1,0:T(8,128)(2,1)S(1)}, bf16[4,56,128]{2,1,0:T(8,128)(2,1)S(1)}, u32[]{:S(2)}, u32[]{:S(2)}) %collective-permute-start.1) | collective-permute-done | bytes 57376 | tf_op jit(solution)/shard_map/ppermute | solution.py:343
  68.2 0.1 join.1
  68.3 10.2 %all_to_all.26 = bf16[4,3,4,56,128]{4,3,2,1,0:T(8,128)(2,1)S(1)} all-to-all(bf16[4,3,4,56,128]{4,3,2,1,0:T(8,128)(2,1)S(1)} %join.1), channel_id=1, replica_groups=mesh['x'=4,'block'=4,'part'=3,'core'=2,'atom'=8] {'x'}, dimensions={0} | all-to-all | bytes 1376256 | tf_op jit(solution)/shard_map/all_to_all | solution.py:347
  78.5 6.6 %collective-permute-start.3 = (bf16[48,56,128]{2,1,0:T(8,128)(2,1)S(1)}, bf16[48,56,128]{2,1,0:T(8,128)(2,1)S(1)}, u32[]{:S(2)}, u32[]{:S(2)}) collective-permute-start(bf16[48,56,128]{2,1,0:T(8,128)(2,1)S(1)} %bitcast.16), channel_id=1, source_target_pairs={{0,8},{8,0},{1,9},{9,1},{2,10},{10,2},{3,11},{11,3},{4,12},{12,4},... | collective-permute-start | bytes 2064392 | tf_op jit(solution)/shard_map/ppermute | solution.py:351
  85.0 2.7 %evaluate.2.refs_0_ = f32[32,128]{1,0:T(8,128)S(1)} custom-call(s32[1]{0:T(128)} %bitcast.half_ref, s32[1,96]{1,0:T(1,128)S(1)} %copy-done.6, bf16[48,56,128]{2,1,0:T(8,128)(2,1)S(1)} %bitcast.17, s32[96,256]{1,0:T(8,128)S(1)} %bitcast.20, s32[96,256]{1,0:T(8,128)S(1)} %bitcast.24, f32[96,256]{1,0:T(8,128)S(1)} %bitcast.28, bf16[49,96,256]{2,1,0:T(8,128)(2,1)S(1)} %bitcast.14), custom_call_target="tpu_custom_call" | custom-call | tf_op jit(solution)/shard_map/evaluate/pallas_call | solution.py:297
  87.7 0.0 collective-permute-done.3.table_ref
  87.7 2.7 %evaluate.3 = f32[32,128]{1,0:T(8,128)S(1)} custom-call(s32[1]{0:T(128)S(6)} %sub.3.half_ref, s32[1,96]{1,0:T(1,128)S(1)} %copy-done.6, bf16[48,56,128]{2,1,0:T(8,128)(2,1)S(1)} %collective-permute-done.3.table_ref, s32[96,256]{1,0:T(8,128)S(1)} %bitcast.21, s32[96,256]{1,0:T(8,128)S(1)} %bitcast.25, f32[96,256]{1,0:T(8,128)S(1)} %bitcast.29, ...), custom_call_target="tpu_custom_call" | custom-call | tf_op jit(solution)/shard_map/evaluate/pallas_call | solution.py:297
  90.4 13.2 %all_to_all.27 = f32[8,1,512]{2,1,0:T(1,128)S(1)} all-to-all(f32[8,1,512]{2,1,0:T(1,128)S(1)} %bitcast.32), channel_id=1, replica_groups=mesh['x'=4,'block'=4,'part'=3,'core'=2,'atom'=8] {'atom'}, dimensions={0} | all-to-all | bytes 32768 | tf_op jit(solution)/shard_map/all_to_all | solution.py:347
  103.6 0.6 reduce_sum.9
  (3 shorter events, 0.0 us)
Async XLA Ops:
  0.0 16.4 %copy-start = (bf16[1,96,49,256]{3,1,2,0:T(8,128)(2,1)S(1)}, bf16[1,96,49,256]{3,1,2,0:T(8,128)(2,1)}, u32[]{:S(2)}) copy-start(bf16[1,96,49,256]{3,1,2,0:T(8,128)(2,1)} %param.12) | copy-start | bytes 7225348
  0.0 16.4 %copy-start.1 = (s32[1,96,256]{2,1,0:T(8,128)S(1)}, s32[1,96,256]{2,1,0:T(8,128)}, u32[]{:S(2)}) copy-start(s32[1,96,256]{2,1,0:T(8,128)} %param.8) | copy-start | bytes 294916
  0.0 16.4 %copy-start.2 = (s32[1,96,256]{2,1,0:T(8,128)S(1)}, s32[1,96,256]{2,1,0:T(8,128)}, u32[]{:S(2)}) copy-start(s32[1,96,256]{2,1,0:T(8,128)} %param.10) | copy-start | bytes 294916
  0.0 16.4 %copy-start.3 = (f32[1,96,256]{2,1,0:T(8,128)S(1)}, f32[1,96,256]{2,1,0:T(8,128)}, u32[]{:S(2)}) copy-start(f32[1,96,256]{2,1,0:T(8,128)} %param.11) | copy-start | bytes 294916
  0.0 16.4 %copy-start.5 = (f32[4096]{0:T(1024)S(1)}, f32[4096]{0:T(1024)}, u32[]{:S(2)}) copy-start(f32[4096]{0:T(1024)} %param.7) | copy-start | bytes 49156
  0.0 16.4 %copy-start.6 = (s32[1,96]{1,0:T(1,128)S(1)}, s32[1,96]{1,0:T(1,128)}, u32[]{:S(2)}) copy-start(s32[1,96]{1,0:T(1,128)} %count_ref.5) | copy-start | bytes 1156
  4.0 15.6 %collective-permute-start = (bf16[48,56,128]{2,1,0:T(8,128)(2,1)S(1)}, bf16[48,56,128]{2,1,0:T(8,128)(2,1)S(1)}, u32[]{:S(2)}, u32[]{:S(2)}) collective-permute-start(bf16[48,56,128]{2,1,0:T(8,128)(2,1)S(1)} %first_moments.1), channel_id=1, source_target_pairs={{0,8},{8,0},{1,9},{9,1},{2,10},{10,2},{3,11},{11,3},{4,12},{12,4},... | collective-permute-start | bytes 2064392 | tf_op jit(solution)/shard_map/ppermute | solution.py:351
  19.8 38.4 %copy-start.4 = (f32[7,128,128]{2,1,0:T(8,128)S(1)}, f32[7,128,128]{2,1,0:T(8,128)}, u32[]{:S(2)}) copy-start(f32[7,128,128]{2,1,0:T(8,128)} %green_ref.1) | copy-start | bytes 1376260
  58.7 5.3 %collective-permute-start.2 = (bf16[4,56,128]{2,1,0:T(8,128)(2,1)S(1)}, bf16[4,56,128]{2,1,0:T(8,128)(2,1)S(1)}, u32[]{:S(2)}, u32[]{:S(2)}) collective-permute-start(bf16[4,56,128]{2,1,0:T(8,128)(2,1)S(1)} %solve.1.own_ref), channel_id=1, source_target_pairs={{0,176},{16,0},{32,16},{48,32},{64,48},{80,64},{96,80},{112,96},{1... | collective-permute-start | bytes 172040 | tf_op jit(solution)/shard_map/ppermute | solution.py:343
  60.6 7.6 %collective-permute-start.1 = (bf16[4,56,128]{2,1,0:T(8,128)(2,1)S(1)}, bf16[4,56,128]{2,1,0:T(8,128)(2,1)S(1)}, u32[]{:S(2)}, u32[]{:S(2)}) collective-permute-start(bf16[4,56,128]{2,1,0:T(8,128)(2,1)S(1)} %solve.1.own_ref), channel_id=1, source_target_pairs={{0,16},{16,32},{32,48},{48,64},{64,80},{80,96},{96,112},{112,128},... | collective-permute-start | bytes 172040 | tf_op jit(solution)/shard_map/ppermute | solution.py:343
  78.5 9.3 %collective-permute-start.3 = (bf16[48,56,128]{2,1,0:T(8,128)(2,1)S(1)}, bf16[48,56,128]{2,1,0:T(8,128)(2,1)S(1)}, u32[]{:S(2)}, u32[]{:S(2)}) collective-permute-start(bf16[48,56,128]{2,1,0:T(8,128)(2,1)S(1)} %bitcast.16), channel_id=1, source_target_pairs={{0,8},{8,0},{1,9},{9,1},{2,10},{10,2},{3,11},{11,3},{4,12},{12,4},... | collective-permute-start | bytes 2064392 | tf_op jit(solution)/shard_map/ppermute | solution.py:351

commit v7 on v5

--- a/solution.py
+++ b/solution.py
@@ -34,19 +34,28 @@
     return jnp.broadcast_to(row, (TILE, SLOTS)).astype(bf16)[None]
 
 
-def hat_rows(grid, index, fraction):
+def hat_parts(index, fraction):
     index = index.astype(f32)
-    upper = jnp.where(grid == tile_of(index + 1.0), tile_of(fraction), jnp.zeros((), bf16))
-    return jnp.where(grid == tile_of(index), tile_of(1.0 - fraction), upper).reshape(R, SLOTS)
-
-
-def one_hot_low(grid, points):
-    low = tile_of((points & (LOW - 1)).astype(f32))
-    return jnp.where(grid == low, jnp.ones((), bf16), jnp.zeros((), bf16)).reshape(LOW, SLOTS)
-
-
-def is_high(points):
-    return lax.broadcasted_iota(jnp.int32, (HIGH, SLOTS), 0) == lax.shift_right_logical(points, 7)
+    return index, index + 1.0, fraction, 1.0 - fraction
+
+
+def hat_rows(grid, parts, i):
+    index, following, fraction, rest = (tile_of(part[i : i + 1, :]) for part in parts)
+    upper = jnp.where(grid == following, fraction, jnp.zeros((), bf16))
+    return jnp.where(grid == index, rest, upper).reshape(R, SLOTS)
+
+
+def one_hot_low(grid, low, i):
+    same = grid == tile_of(low[i : i + 1, :])
+    return jnp.where(same, jnp.ones((), bf16), jnp.zeros((), bf16)).reshape(LOW, SLOTS)
+
+
+def low_of(points):
+    return (points & (LOW - 1)).astype(f32)
+
+
+def high_of(points):
+    return lax.shift_right_logical(points, 7)
 
 
 def add_moments(base, counts, tasks, angular_rows, rho_ref, out_ref, left_ref, right_ref):
@@ -58,10 +67,13 @@
     slot = lax.broadcasted_iota(jnp.int32, (1, SLOTS), 1)
     grid = radial_grid()
     densities = []
+    lows, highs = low_of(points), high_of(points)
+    parts = hat_parts(index, fraction)
+    high_grid = lax.broadcasted_iota(jnp.int32, (HIGH, SLOTS), 0)
     for i in range(BLOCK):
-        low = one_hot_low(grid, points[i : i + 1, :])
+        low = one_hot_low(grid, lows, i)
         columns = jnp.dot(rho_parts, jnp.concatenate([low, low], axis=0), preferred_element_type=f32)
-        picked = jnp.sum(jnp.where(is_high(points[i : i + 1, :]), columns, 0.0), axis=0, keepdims=True)
+        picked = jnp.sum(jnp.where(high_grid == highs[i : i + 1, :], columns, 0.0), axis=0, keepdims=True)
         densities.append(jnp.where(slot < counts(i), picked, 0.0))
     densities = jnp.concatenate(densities, axis=0)
     for m, angular in enumerate(angular_rows()):
@@ -71,7 +83,7 @@
     for i in range(BLOCK):
         of_atom = pl.ds(i, ROWS, stride=BLOCK)
         weighted = jnp.concatenate([left_ref[of_atom, :], right_ref[of_atom, :]], axis=1).astype(bf16)
-        rows = hat_rows(grid, index[i : i + 1, :], fraction[i : i + 1, :])
+        rows = hat_rows(grid, parts, i)
         out_ref[base + i] = lax.dot_general(
             weighted, rows, (((1,), (1,)), ((), ())), preferred_element_type=f32
         ).astype(out_ref.dtype)
@@ -187,8 +199,9 @@
         points = point_ref[pl.ds(start, BLOCK), :]
         index = index_ref[pl.ds(start, BLOCK), :]
         fraction = fraction_ref[pl.ds(start, BLOCK), :]
+        parts = hat_parts(index, fraction)
         for i in range(BLOCK):
-            rows = hat_rows(grid, index[i : i + 1, :], fraction[i : i + 1, :])
+            rows = hat_rows(grid, parts, i)
             radial = jnp.dot(table_ref[base + i], rows, preferred_element_type=f32)
             of_atom = pl.ds(i, ROWS, stride=BLOCK)
             left_ref[of_atom, :] = radial[:, :LANES]
@@ -201,15 +214,21 @@
                 sums[m % 2] = sums[m % 2] + angular * radial_ref[m * BLOCK : (m + 1) * BLOCK, :]
             values.append(sums[0] + sums[1])
         values = jnp.concatenate(values, axis=1)
+        lows, highs = low_of(points), high_of(points).astype(f32)
+        bigs = values.astype(bf16).astype(f32)
+        smalls = values - bigs
+        none = jnp.zeros((), bf16)
         for i in range(BLOCK):
-            value = jnp.where(slot < count_ref[0, start + i], values[i : i + 1, :], 0.0)
-            big = value.astype(bf16).astype(f32)
-            small = value - big
-            high = is_high(points[i : i + 1, :])
-            spread = jnp.concatenate([jnp.where(high, big, 0.0), jnp.where(high, small, 0.0)], axis=0)
-            low = one_hot_low(grid, points[i : i + 1, :])
+            live = slot < count_ref[0, start + i]
+            big = tile_of(jnp.where(live, bigs[i : i + 1, :], 0.0))
+            small = tile_of(jnp.where(live, smalls[i : i + 1, :], 0.0))
+            high = grid[: HIGH // TILE] == tile_of(highs[i : i + 1, :])
+            spread = jnp.concatenate([jnp.where(high, big, none), jnp.where(high, small, none)], axis=0)
             total = total + lax.dot_general(
-                spread.astype(bf16), low, (((1,), (1,)), ((), ())), preferred_element_type=f32
+                spread.reshape(2 * HIGH, SLOTS),
+                one_hot_low(grid, lows, i),
+                (((1,), (1,)), ((), ())),
+                preferred_element_type=f32,
             )
         return total
 

time: 99.2 us -> 99.4 us (level)
  no operation moved by 1% of the time
where the time goes in v7:
time: 99.4 us; the launch traced here: 99.1 us
  blocking collectives  64.6 us (65%)
  starting transfers between devices  20.3 us (20%)
  Pallas kernels  13.2 us (13%)
    all_to_all x4, blocking collectives, exchanged(): return lax.all_to_all(array, axis, split_axis=0, concat_axis=0, tiled=True)  64.6 us
    ppermute x2, starting transfers between devices, to_other_core(): return lax.ppermute(array, 'core', [(0, 1), (1, 0)])  20.3 us
    pallas_call x2, Pallas kernels, evaluated(): pl.pallas_call(evaluate_kernel, out_shape=pltpu.VMEM((HIGH, LOW), f32), i...  5.51 us
    pallas_call x1, Pallas kernels, first_moments_of(): pl.pallas_call(first_moments_kernel, out_shape=pltpu.VMEM((HALF, ROWS, R)...  3.99 us
    pallas_call x1, Pallas kernels, moments_of(): pl.pallas_call(moments_kernel, out_shape=pltpu.VMEM((HALF, ROWS, R), f32)...  3.12 us
  transfers between devices with their start and end apart: 2, of which 0 were waited for; matrix products, arithmetic and copies ran while one was open for 0% of the time, Pallas kernels for 6%

profile of v7, /device:TPU:1, one launch (start us, length us, event | category | flops | bytes accessed | tf_op | source)
XLA Modules:
  0.0 99.1 jit_solution(1405186641589502830)
XLA Ops:
  0.0 0.0 copy-start
  0.0 0.0 copy-start.1
  0.0 0.0 copy-start.2
  0.0 0.0 copy-start.3
  0.0 0.0 copy-start.5
  0.0 0.0 copy-start.6
  0.0 4.0 %first_moments.1 = bf16[48,56,128]{2,1,0:T(8,128)(2,1)S(1)} custom-call(s32[1]{0:T(128)S(6)} %sub.3.half_ref, s32[1,96]{1,0:T(1,128)} %count_ref.5, f32[32,128]{1,0:T(8,128)} %bitcast.29, s32[96,256]{1,0:T(8,128)} %bitcast.17, s32[96,256]{1,0:T(8,128)} %bitcast.21, f32[96,256]{1,0:T(8,128)} %bitcast.25, bf16[49,96,256]{2,1,0:T(8,128)(2,1)} %bitcast.11), custom_call_target="tpu_custom_call" | custom-call | tf_op jit(solution)/shard_map/first_moments/pallas_call | solution.py:274
  4.0 12.4 %collective-permute-start = (bf16[48,56,128]{2,1,0:T(8,128)(2,1)S(1)}, bf16[48,56,128]{2,1,0:T(8,128)(2,1)S(1)}, u32[]{:S(2)}, u32[]{:S(2)}) collective-permute-start(bf16[48,56,128]{2,1,0:T(8,128)(2,1)S(1)} %first_moments.1), channel_id=1, source_target_pairs={{0,8},{8,0},{1,9},{9,1},{2,10},{10,2},{3,11},{11,3},{4,12},{12,4},... | collective-permute-start | bytes 2064392 | tf_op jit(solution)/shard_map/ppermute | solution.py:347
  16.4 0.0 copy-done
  16.4 0.0 copy-done.1
  16.4 0.0 copy-done.2
  16.5 0.0 copy-done.3
  16.5 0.0 copy-done.5
  16.5 0.0 copy-done.6
  16.5 3.1 %moments.1 = f32[48,56,128]{2,1,0:T(8,128)S(1)} custom-call(s32[1]{0:T(128)} %bitcast.half_ref, s32[1,96]{1,0:T(1,128)S(1)} %copy-done.6, f32[32,128]{1,0:T(8,128)S(1)} %bitcast.30, s32[96,256]{1,0:T(8,128)S(1)} %bitcast.18, s32[96,256]{1,0:T(8,128)S(1)} %bitcast.22, f32[96,256]{1,0:T(8,128)S(1)} %bitcast.26, bf16[49,96,256]{2,1,0:T(8,128)(2,1)S(1)} %bitcast.12), custom_call_target="tpu_custom_call" | custom-call | tf_op jit(solution)/shard_map/moments/pallas_call | solution.py:297
  19.6 0.0 collective-permute-done
  19.6 0.2 add_convert_fusion
  19.8 0.0 copy-start.4
  19.8 17.4 %all_to_all.24.arrived_ref = bf16[12,4,56,128]{3,2,1,0:T(8,128)(2,1)S(1)} all-to-all(bf16[12,4,56,128]{3,2,1,0:T(8,128)(2,1)S(1)} %bitcast.32), channel_id=1, replica_groups=mesh['x'=4,'block'=4,'part'=3,'core'=2,'atom'=8] {'x','part'}, dimensions={0} | all-to-all | bytes 1376256 | tf_op jit(solution)/shard_map/all_to_all | solution.py:343
  37.2 0.1 sum.1
  37.3 20.9 %all_to_all.25.parts_ref = bf16[4,4,56,128]{3,2,1,0:T(8,128)(2,1)S(1)} all-to-all(bf16[4,4,56,128]{3,2,1,0:T(8,128)(2,1)S(1)} %sum.1), channel_id=1, replica_groups=mesh['x'=4,'block'=4,'part'=3,'core'=2,'atom'=8] {'block'}, dimensions={0} | all-to-all | bytes 458752 | tf_op jit(solution)/shard_map/all_to_all | solution.py:343
  58.2 0.0 copy-done.4
  58.2 0.5 solve.1
  58.7 13.1 %all_to_all.26 = bf16[12,4,56,128]{3,2,1,0:T(8,128)(2,1)S(1)} all-to-all(bf16[12,4,56,128]{3,2,1,0:T(8,128)(2,1)S(1)} %solve.1), channel_id=1, replica_groups=mesh['x'=4,'block'=4,'part'=3,'core'=2,'atom'=8] {'x','part'}, dimensions={0} | all-to-all | bytes 1376256 | tf_op jit(solution)/shard_map/all_to_all | solution.py:343
  71.8 7.9 %collective-permute-start.1 = (bf16[48,56,128]{2,1,0:T(8,128)(2,1)S(1)}, bf16[48,56,128]{2,1,0:T(8,128)(2,1)S(1)}, u32[]{:S(2)}, u32[]{:S(2)}) collective-permute-start(bf16[48,56,128]{2,1,0:T(8,128)(2,1)S(1)} %bitcast.15), channel_id=1, source_target_pairs={{0,8},{8,0},{1,9},{9,1},{2,10},{10,2},{3,11},{11,3},{4,12},{12,4},... | collective-permute-start | bytes 2064392 | tf_op jit(solution)/shard_map/ppermute | solution.py:347
  79.7 2.7 %evaluate.2.refs_0_ = f32[32,128]{1,0:T(8,128)S(1)} custom-call(s32[1]{0:T(128)} %bitcast.half_ref, s32[1,96]{1,0:T(1,128)S(1)} %copy-done.6, bf16[48,56,128]{2,1,0:T(8,128)(2,1)S(1)} %bitcast.16, s32[96,256]{1,0:T(8,128)S(1)} %bitcast.19, s32[96,256]{1,0:T(8,128)S(1)} %bitcast.23, f32[96,256]{1,0:T(8,128)S(1)} %bitcast.27, bf16[49,96,256]{2,1,0:T(8,128)(2,1)S(1)} %bitcast.13), custom_call_target="tpu_custom_call" | custom-call | tf_op jit(solution)/shard_map/evaluate/pallas_call | solution.py:309
  82.5 0.0 collective-permute-done.1.table_ref
  82.5 2.8 %evaluate.3 = f32[32,128]{1,0:T(8,128)S(1)} custom-call(s32[1]{0:T(128)S(6)} %sub.3.half_ref, s32[1,96]{1,0:T(1,128)S(1)} %copy-done.6, bf16[48,56,128]{2,1,0:T(8,128)(2,1)S(1)} %collective-permute-done.1.table_ref, s32[96,256]{1,0:T(8,128)S(1)} %bitcast.20, s32[96,256]{1,0:T(8,128)S(1)} %bitcast.24, f32[96,256]{1,0:T(8,128)S(1)} %bitcast.28, ...), custom_call_target="tpu_custom_call" | custom-call | tf_op jit(solution)/shard_map/evaluate/pallas_call | solution.py:309
  85.3 13.2 %all_to_all.27 = f32[8,1,512]{2,1,0:T(1,128)S(1)} all-to-all(f32[8,1,512]{2,1,0:T(1,128)S(1)} %bitcast.31), channel_id=1, replica_groups=mesh['x'=4,'block'=4,'part'=3,'core'=2,'atom'=8] {'atom'}, dimensions={0} | all-to-all | bytes 32768 | tf_op jit(solution)/shard_map/all_to_all | solution.py:343
  98.5 0.6 reduce_sum.9
Async XLA Ops:
  0.0 16.4 %copy-start = (bf16[1,96,49,256]{3,1,2,0:T(8,128)(2,1)S(1)}, bf16[1,96,49,256]{3,1,2,0:T(8,128)(2,1)}, u32[]{:S(2)}) copy-start(bf16[1,96,49,256]{3,1,2,0:T(8,128)(2,1)} %param.12) | copy-start | bytes 7225348
  0.0 16.4 %copy-start.1 = (s32[1,96,256]{2,1,0:T(8,128)S(1)}, s32[1,96,256]{2,1,0:T(8,128)}, u32[]{:S(2)}) copy-start(s32[1,96,256]{2,1,0:T(8,128)} %param.8) | copy-start | bytes 294916
  0.0 16.4 %copy-start.2 = (s32[1,96,256]{2,1,0:T(8,128)S(1)}, s32[1,96,256]{2,1,0:T(8,128)}, u32[]{:S(2)}) copy-start(s32[1,96,256]{2,1,0:T(8,128)} %param.10) | copy-start | bytes 294916
  0.0 16.4 %copy-start.3 = (f32[1,96,256]{2,1,0:T(8,128)S(1)}, f32[1,96,256]{2,1,0:T(8,128)}, u32[]{:S(2)}) copy-start(f32[1,96,256]{2,1,0:T(8,128)} %param.11) | copy-start | bytes 294916
  0.0 16.4 %copy-start.5 = (f32[4096]{0:T(1024)S(1)}, f32[4096]{0:T(1024)}, u32[]{:S(2)}) copy-start(f32[4096]{0:T(1024)} %param.7) | copy-start | bytes 49156
  0.0 16.4 %copy-start.6 = (s32[1,96]{1,0:T(1,128)S(1)}, s32[1,96]{1,0:T(1,128)}, u32[]{:S(2)}) copy-start(s32[1,96]{1,0:T(1,128)} %count_ref.5) | copy-start | bytes 1156
  4.0 15.6 %collective-permute-start = (bf16[48,56,128]{2,1,0:T(8,128)(2,1)S(1)}, bf16[48,56,128]{2,1,0:T(8,128)(2,1)S(1)}, u32[]{:S(2)}, u32[]{:S(2)}) collective-permute-start(bf16[48,56,128]{2,1,0:T(8,128)(2,1)S(1)} %first_moments.1), channel_id=1, source_target_pairs={{0,8},{8,0},{1,9},{9,1},{2,10},{10,2},{3,11},{11,3},{4,12},{12,4},... | collective-permute-start | bytes 2064392 | tf_op jit(solution)/shard_map/ppermute | solution.py:347
  19.8 38.4 %copy-start.4 = (f32[7,128,128]{2,1,0:T(8,128)S(1)}, f32[7,128,128]{2,1,0:T(8,128)}, u32[]{:S(2)}) copy-start(f32[7,128,128]{2,1,0:T(8,128)} %green_ref.1) | copy-start | bytes 1376260
  71.8 10.7 %collective-permute-start.1 = (bf16[48,56,128]{2,1,0:T(8,128)(2,1)S(1)}, bf16[48,56,128]{2,1,0:T(8,128)(2,1)S(1)}, u32[]{:S(2)}, u32[]{:S(2)}) collective-permute-start(bf16[48,56,128]{2,1,0:T(8,128)(2,1)S(1)} %bitcast.15), channel_id=1, source_target_pairs={{0,8},{8,0},{1,9},{9,1},{2,10},{10,2},{3,11},{11,3},{4,12},{12,4},... | collective-permute-start | bytes 2064392 | tf_op jit(solution)/shard_map/ppermute | solution.py:347
